TPU v7x, 1024 devices: a whole 4x8x16 slice. The times are simulated.
1024 devices in a mesh: dp: 64 (over z, x), fsdp: 16 (over y, core).
Axes of the slice: x: 4, y: 8, z: 16, core: 2. Of those that a mesh axis runs over, the one named last changes fastest.
Arguments:
- text_states: bfloat16 [192, 64, 4096], P('dp', None, 'fsdp'), may hold values from -6 to 6
- cotangent: bfloat16 [192, 64, 4096], P('dp', None, 'fsdp'), may hold values from -16 to 16
- norm_gain: float32 [4096], replicated, may hold values from 0.5 to 120
- norm_bias: float32 [4096], replicated, may hold values from -3 to 3
- branch_gate: float32 [1], replicated, may hold values from 0.4 to 1.2
- query_weight: bfloat16 [4096, 16, 128], P(None, 'fsdp'), may hold values from -0.09375 to 0.09375
- latent_weight: bfloat16 [4096, 16, 256], P(None, 'fsdp'), may hold values from -0.09375 to 0.09375
- output_weight: bfloat16 [16, 128, 4096], P('fsdp'), may hold values from -0.125 to 0.125
- latents: bfloat16 [576, 64, 4096], P('dp'), may hold values from -6 to 6
- media_refs: int32 [192, 5], replicated, may hold values from -1 to 575, as said below
- media_pos: int32 [192, 64], P('dp'), may hold values from -1 to 4, as said below
- owner_map: int32 [576], replicated, may hold values from 0 to 575, as said below
Outputs:
- layer_out: bfloat16 [192, 64, 4096], P('dp', None, 'fsdp')
- out_grad: float32 [16, 128, 4096], P('fsdp', None, 'dp')
Inputs may be any that keep to these rules, and one draw needn't show every extreme that they name: `media_refs`: row s holds the ids of sequence s's images in its first 1 to 5 entries, the rest are -1; every image id stands in exactly one row. A permutation: image i's latents are storage row owner_map[i], held by data shard owner_map[i] // 9. The images of one data shard's sequences lie on at most 1 storage rows of any one data shard, and some data shard reaches 1. `media_pos`: for each token, the number of its sequence's images placed at or before it, minus one; images take increasing positions in the window, each image has tokens, and a slot named is always filled in media_refs.
All inputs are finite; a program needn't handle non-finite values.
Results may differ from a plain program's by a relative error of at most 0.039.
The roundings to bfloat16 on the way count: a program that leaves them out, or rounds other values in their place, can miss the bound.
Values may be sent and summed in bfloat16 or wider, within the bound.
A program may use at most 64 MiB of HBM per device.

v0:
```python
import jax
import jax.numpy as jnp
from jax import lax
from jax.sharding import Mesh
from jax.sharding import PartitionSpec as P

DP = ("dp_0", "dp_1")


EPSILON = 1e-05


def side_by_side(arrays, axis, dim, along):
    both = jnp.concatenate(arrays, axis=along)
    result, at, outs = (lax.all_gather(both, axis, axis=dim, tiled=True), 0, [])
    for a in arrays:
        outs.append(lax.slice_in_dim(result, at, at + a.shape[along], axis=along))
        at += a.shape[along]
    return tuple(outs)


def reduced_to_own(pieces, axes, turns):
    dims = [lax.axis_size(a) for a in axes]
    pieces = pieces.reshape(*dims, *pieces.shape[1:])
    pieces = pieces.transpose(*turns, *range(len(axes), pieces.ndim))
    pieces = pieces.reshape(-1, *pieces.shape[len(axes) :])
    for k in turns:
        pieces = lax.psum_scatter(pieces, axes[k], scatter_dimension=0, tiled=True)
    return pieces[0]


def cut_along(value, dim, peers):
    before, after = (value.shape[:dim], value.shape[dim + 1 :])
    return jnp.moveaxis(value.reshape(*before, peers, -1, *after), dim, 0)


def sum_by_axis(value, axes, turns, dim):
    peers = lax.axis_size(axes)
    return reduced_to_own(cut_along(value, dim, peers), axes, turns)


def layer_norm(row_values, norm_gain, norm_bias):
    as_float = row_values.astype(jnp.float32)
    row_mean = jnp.mean(as_float, axis=-1, keepdims=True)
    centered = as_float - row_mean
    variance = jnp.mean(centered * centered, axis=-1, keepdims=True)
    return (centered * lax.rsqrt(variance + EPSILON) * norm_gain + norm_bias).astype(jnp.bfloat16)


def body(
    text_states,
    cotangent,
    norm_gain,
    norm_bias,
    branch_gate,
    query_weight,
    latent_weight,
    output_weight,
    latents,
    media_refs,
    media_pos,
    owner_map,
):
    seq_local, window, feat_local = text_states.shape
    model_width = query_weight.shape[0]
    head_local, head_size = (query_weight.shape[1], query_weight.shape[2])
    pair_width = head_local * 2 * head_size
    img_local, latent_rows = (latents.shape[0], latents.shape[1])
    groups = lax.axis_size(DP)
    my_group = lax.axis_index(DP)
    per_sequence = media_refs.shape[1]
    slot_count = media_refs.shape[0] * per_sequence // groups
    capacity = (slot_count + groups - 1) // groups
    images = owner_map.shape[0]
    gate_scale = jnp.tanh(branch_gate[0])
    own_pairs = jnp.dot(
        latents.reshape(img_local * latent_rows, model_width),
        latent_weight.reshape(model_width, pair_width),
        preferred_element_type=jnp.float32,
    )
    own_pairs = own_pairs.astype(jnp.bfloat16).reshape(img_local, latent_rows, pair_width)
    group_refs = media_refs.reshape(groups, slot_count)
    present = group_refs >= 0
    lookup = jnp.maximum(group_refs, 0)[:, :, None] == jnp.arange(images, dtype=jnp.int32)
    storage = jnp.sum(jnp.where(lookup, owner_map, 0), axis=-1)
    source = storage // img_local
    within = storage % img_local
    position = jnp.arange(slot_count, dtype=jnp.int32)
    earlier = (
        (source[:, :, None] == source[:, None, :])
        & present[:, None, :]
        & (position[None, None, :] < position[None, :, None])
    )
    before = jnp.sum(earlier.astype(jnp.int32), axis=-1)
    owned_here = present & (source == my_group)
    chosen = owned_here[:, None, :] & (
        before[:, None, :] == jnp.arange(capacity, dtype=jnp.int32)[None, :, None]
    )
    filled = jnp.any(chosen, axis=-1).reshape(-1)
    picked = jnp.sum(jnp.where(chosen, within[:, None, :], 0), axis=-1).reshape(-1)
    outgoing = jnp.where(filled[:, None, None], own_pairs[picked], jnp.zeros((), jnp.bfloat16))
    incoming = lax.all_to_all(outgoing, DP, split_axis=0, concat_axis=0, tiled=True)
    own_source = lax.dynamic_index_in_dim(source, my_group, 0, keepdims=False)
    own_before = lax.dynamic_index_in_dim(before, my_group, 0, keepdims=False)
    arrival = jnp.clip(own_source * capacity + own_before, 0, groups * capacity - 1)
    arrived_pairs = incoming[arrival].reshape(
        seq_local, per_sequence * latent_rows, head_local, 2 * head_size
    )
    text_rows, upstream = side_by_side((text_states, cotangent), "fsdp", 2, 0)
    tokens = seq_local * window
    normed = layer_norm(text_rows.reshape(tokens, model_width), norm_gain, norm_bias)
    queries = jnp.dot(
        normed,
        query_weight.reshape(model_width, head_local * head_size),
        preferred_element_type=jnp.float32,
    )
    queries = (
        (queries * head_size ** (-0.5))
        .astype(jnp.bfloat16)
        .reshape(seq_local, window, head_local, head_size)
    )
    key_part = arrived_pairs[..., :head_size]
    value_part = arrived_pairs[..., head_size:]
    scores = jnp.einsum("sthe,smhe->shtm", queries, key_part, preferred_element_type=jnp.float32)
    column_image = jnp.arange(per_sequence * latent_rows, dtype=jnp.int32) // latent_rows
    allowed = media_pos[:, :, None] == column_image
    scores = jnp.where(allowed[:, None], scores, -1e30)
    row_max = jnp.max(scores, axis=-1, keepdims=True)
    weights = jnp.exp(scores - row_max)
    softmaxed = (weights / jnp.sum(weights, axis=-1, keepdims=True)).astype(jnp.bfloat16)
    context = jnp.einsum(
        "shtm,smhe->sthe", softmaxed, value_part, preferred_element_type=jnp.float32
    )
    context = jnp.where(media_pos[:, :, None, None] >= 0, context, 0.0).astype(jnp.bfloat16)
    context_rows = context.reshape(tokens, head_local * head_size)
    out_rows = output_weight.reshape(head_local * head_size, model_width)
    update = lax.psum_scatter(
        lax.dot_general(
            out_rows, context_rows, (((0,), (1,)), ((), ())), preferred_element_type=jnp.float32
        ),
        "fsdp",
        scatter_dimension=0,
        tiled=True,
    )
    update = jnp.transpose(update, (1, 0))
    update = update.reshape(seq_local, window, feat_local)
    layer_out = (text_states.astype(jnp.float32) + gate_scale * update).astype(jnp.bfloat16)
    local_grad = gate_scale * jnp.einsum(
        "te,td->ed",
        context_rows,
        upstream.reshape(tokens, model_width),
        preferred_element_type=jnp.float32,
    )
    out_grad = sum_by_axis(local_grad.reshape(head_local, head_size, model_width), DP, (1, 0), 2)
    return (layer_out, out_grad)


def solution(mesh):
    split = Mesh(mesh.devices.reshape(16, 4, mesh.shape["fsdp"]), ("dp_0", "dp_1", "fsdp"))
    return jax.shard_map(
        body,
        mesh=split,
        in_specs=(
            P(DP, None, "fsdp"),
            P(DP, None, "fsdp"),
            P(),
            P(),
            P(),
            P(None, "fsdp", None),
            P(None, "fsdp", None),
            P("fsdp", None, None),
            P(DP, None, None),
            P(),
            P(DP, None),
            P(),
        ),
        out_specs=(P(DP, None, "fsdp"), P("fsdp", None, DP)),
        check_vma=False,
    )
```

profile of v0, /device:TPU:6, one launch (start us, length us, event | category | flops | bytes accessed | tf_op | source)
XLA Modules:
  0.0 343.6 jit_solution(2178677289342070783)
XLA Ops:
  7.2 0.8 broadcast_maximum_fusion
  8.0 0.7 broadcast_compare_fusion
  8.7 0.2 copy.28
  9.4 1.3 select_reduce_fusion
  10.9 0.1 convert_reduce_fusion.1
  11.1 3.7 %fusion.10 = bf16[576,256]{1,0:T(8,128)(2,1)S(1)} fusion(bf16[576,4096]{1,0:T(8,128)(2,1)} %bitcast.102, bf16[4096,1,256]{2,0,1:T(8,128)(2,1)S(1)} %copy-done), kind=kOutput, calls=%fused_computation.19 | convolution fusion | flops 1208107008 | bytes 7110656 | tf_op jit(solution)/shard_map/dot_general | solution.py:76
  14.9 2.0 gather_fusion
  16.9 3.2 broadcast_select_fusion
  20.1 22.6 %all-to-all-start = ((bf16[64,64,256]{2,1,0:T(8,128)(2,1)}), bf16[64,64,256]{2,1,0:T(8,128)(2,1)}, u32[]{:S(2)}, u32[]{:S(2)}) async-start(bf16[64,64,256]{2,1,0:T(8,128)(2,1)} %broadcast_select_fusion), calls=%async_computation | async-start | bytes 4194304 | tf_op jit(solution)/shard_map/all_to_all | solution.py:102
  42.7 0.7 pad_maximum_fusion
  44.2 0.2 clamp_reduce_fusion
  44.5 54.7 %all-gather.2.cloned.1.call-done = bf16[6,64,4096]{2,1,0:T(8,128)(2,1)} async-done(((bf16[6,64,256]{2,1,0:T(8,128)(2,1)}), bf16[6,64,4096]{2,1,0:T(8,128)(2,1)}) %all-gather.2.cloned.1.call-update) | async-done | bytes 3145744 | tf_op jit(solution)/shard_map/all_gather | solution.py:15
  99.1 2.9 slice.23
  102.1 0.3 convert_reduce_fusion
  102.4 0.6 fusion.3
  103.0 0.7 fusion.6
  103.7 0.6 fusion.14
  104.3 38.5 %all-to-all-done = bf16[64,64,256]{2,1,0:T(8,128)(2,1)} async-done(((bf16[64,64,256]{2,1,0:T(8,128)(2,1)}), bf16[64,64,256]{2,1,0:T(8,128)(2,1)}, u32[]{:S(2)}, u32[]{:S(2)}) %all-to-all-start) | async-done | bytes 2097184 | tf_op jit(solution)/shard_map/all_to_all | solution.py:102
  142.7 2.2 gather_fusion.1
  144.9 0.2 convolution_select_fusion
  145.1 0.2 fusion.34
  145.3 0.4 fusion.16
  145.8 3.2 convolution_multiply_fusion
  149.0 2.9 copy.34
  151.9 3.2 copy.35
  155.2 1.1 copy-done.3
  156.4 2.2 convolution_bitcast_fusion
  158.7 26.5 %reduce-scatter.6.cloned.1.call-done = f32[16,1,128,64]{2,3,1,0:T(8,128)} async-done(((f32[64,1,128,64]{2,3,1,0:T(8,128)}), f32[16,1,128,64]{2,3,1,0:T(8,128)}) %reduce-scatter.6.cloned.1.call-update) | async-done | bytes 524304 | tf_op jit(solution)/shard_map/reduce_scatter | solution.py:28
  185.2 74.5 %reduce-scatter.4.cloned.1.call-done = f32[256,192]{0,1:T(8,128)} async-done(((f32[4096,192]{0,1:T(8,128)}), f32[256,192]{0,1:T(8,128)}) %reduce-scatter.4.cloned.1.call-update) | async-done | bytes 196624 | tf_op jit(solution)/shard_map/reduce_scatter | solution.py:137
  259.8 0.9 broadcast_multiply_fusion
  260.7 0.7 add_convert_fusion
  261.4 75.7 %reduce-scatter.8.cloned.1.call-done = f32[1,1,128,64]{2,3,1,0:T(8,128)} async-done(((f32[16,1,128,64]{2,3,1,0:T(8,128)}), f32[1,1,128,64]{2,3,1,0:T(8,128)}) %reduce-scatter.8.cloned.1.call-update) | async-done | bytes 32784 | tf_op jit(solution)/shard_map/reduce_scatter | solution.py:28
  (44 shorter events, 1.1 us)
Async XLA Ops:
  7.2 4.0 %copy-start = (bf16[4096,1,256]{2,0,1:T(8,128)(2,1)S(1)}, bf16[4096,1,256]{2,0,1:T(8,128)(2,1)}, u32[]{:S(2)}) copy-start(bf16[4096,1,256]{2,0,1:T(8,128)(2,1)} %param.18) | copy-start | bytes 6291460
  20.1 22.6 %copy-start.4 = (bf16[3,64,256]{2,1,0:T(8,128)(2,1)S(1)}, bf16[3,64,256]{2,1,0:T(8,128)(2,1)}, u32[]{:S(2)}) copy-start(bf16[3,64,256]{2,1,0:T(8,128)(2,1)} %param.12) | copy-start | bytes 294916
  20.1 22.7 %copy-start.5 = (bf16[3,64,256]{2,1,0:T(8,128)(2,1)S(1)}, bf16[3,64,256]{2,1,0:T(8,128)(2,1)}, u32[]{:S(2)}) copy-start(bf16[3,64,256]{2,1,0:T(8,128)(2,1)} %param.13) | copy-start | bytes 294916
  20.1 24.3 %copy-start.8 = (s32[3,64]{1,0:T(4,128)S(1)}, s32[3,64]{1,0:T(4,128)}, u32[]{:S(2)}) copy-start(s32[3,64]{1,0:T(4,128)} %param.22) | copy-start | bytes 2308
  20.1 122.6 %all-to-all-start = ((bf16[64,64,256]{2,1,0:T(8,128)(2,1)}), bf16[64,64,256]{2,1,0:T(8,128)(2,1)}, u32[]{:S(2)}, u32[]{:S(2)}) async-start(bf16[64,64,256]{2,1,0:T(8,128)(2,1)} %broadcast_select_fusion), calls=%async_computation | async-start | bytes 4194304 | tf_op jit(solution)/shard_map/all_to_all | solution.py:102
  42.7 56.5 %all-gather.2.cloned.1.call-start = ((), (), s32[]{:S(2)}) async-start(), calls=%async_computation.4 | async-start | bytes 3342336 | tf_op jit(solution)/shard_map/all_gather | solution.py:15
  43.5 141.7 %reduce-scatter.6.cloned.1.call-start = ((), (), s32[]{:S(2)}) async-start(), calls=%async_computation.6 | async-start | bytes 2621440 | tf_op jit(solution)/shard_map/reduce_scatter | solution.py:28
  99.1 2.9 copy-start.1
  102.1 0.9 copy-start.6
  102.1 0.9 copy-start.7
  102.4 1.3 copy-start.2
  155.1 1.2 copy-start.3
  155.2 104.6 %reduce-scatter.4.cloned.1.call-start = ((), (), s32[]{:S(2)}) async-start(), calls=%async_computation.5 | async-start | bytes 3342336 | tf_op jit(solution)/shard_map/reduce_scatter | solution.py:137
  158.6 178.4 %reduce-scatter.8.cloned.1.call-start = ((), (), s32[]{:S(2)}) async-start(), calls=%async_computation.7 | async-start | bytes 557056 | tf_op jit(solution)/shard_map/reduce_scatter | solution.py:28
Sparse Core Ops, SparseCore 0:
  46.1 52.9 all-gather.1
  155.3 29.8 reduce-scatter.5
  188.6 71.0 reduce-scatter.3
  263.6 73.4 reduce-scatter.7
where the time goes:
time: 344 us
  waiting for transfers between devices  270 us (78%)
  starting transfers between devices  22.7 us (7%)
  local copies, waits for them, and re-layouts  15.3 us (4%)
  between operations  14.6 us (4%)
  other arithmetic  10.6 us (3%)
  matrix products  10.4 us (3%)
    reduce_scatter x2, waiting for transfers between devices, reduced_to_own(): pieces = lax.psum_scatter(pieces, axes[k], scatter_dimension=0, tiled=True)  102 us
    reduce_scatter x1, waiting for transfers between devices, body(): lax.psum_scatter(lax.dot_general(out_rows, context_rows, (((0,), (1,)), (...  74.5 us
    all_gather x1, waiting for transfers between devices, side_by_side(): result, at, outs = (lax.all_gather(both, axis, axis=dim, tiled=True), 0, [])  54.7 us
    all_to_all x1, waiting for transfers between devices, body(): lax.all_to_all(outgoing, DP, split_axis=0, concat_axis=0, tiled=True)  38.5 us
    all_to_all x1, starting transfers between devices, body(): lax.all_to_all(outgoing, DP, split_axis=0, concat_axis=0, tiled=True)  22.6 us
  transfers between devices with their start and end apart: 5, of which 5 were waited for; matrix products, arithmetic and copies ran while one was open for 3% of the time, Pallas kernels for 0%

commit v1 on v0

v1 whole, which is shorter than its diff:
```python
import functools

import jax
import jax.numpy as jnp
from jax import lax
from jax.experimental import pallas as pl
from jax.experimental.pallas import tpu as pltpu
from jax.sharding import Mesh
from jax.sharding import PartitionSpec as P

EPSILON = 1e-05
MESH = pl.DeviceIdType.MESH
NZ, NX, NY = 16, 4, 8
GROUP = 2 * NY
IMG = 9
LAT = 64
TOK = 192
CHUNKS = 3
CHUNK_ROWS = IMG * LAT // CHUNKS
HALF_Z = NZ // 2
HALF_Y = NY // 2
BF16 = jnp.bfloat16
F32 = jnp.float32


def remote(src, dst, send, recv, where):
    return pltpu.make_async_remote_copy(
        src_ref=src, dst_ref=dst, send_sem=send, recv_sem=recv, device_id=where, device_id_type=MESH
    )


def position():
    return lax.axis_index("z"), lax.axis_index("x"), lax.axis_index("y"), lax.axis_index("c")


def meet(targets):
    barrier = pltpu.get_barrier_semaphore()
    for where in targets:
        pl.semaphore_signal(barrier, inc=1, device_id=where, device_id_type=MESH)
    return lambda: pl.semaphore_wait(barrier, len(targets))


def fsdp_peers(y, c):
    peers = [{"c": 1 - c}]
    for dy in range(1, NY):
        for dc in range(2):
            peers.append({"y": lax.rem(y + dy, NY), "c": lax.rem(c + dc, 2)})
    return peers


def x_peers(x):
    return [{"x": lax.rem(x + dx, NX)} for dx in range(1, NX)]


class YRing:
    def __init__(self, own, full, y, c, send, recv, psend, precv):
        self.own, self.full, self.y, self.c = own, full, y, c
        self.send, self.recv, self.psend, self.precv = send, recv, psend, precv
        self.started = []

    def slot(self, direction, k, core):
        row = lax.rem(self.y + (NY - k if direction == 0 else k), NY)
        return self.full.at[2 * row + core]

    def neighbour(self, direction):
        return {"y": lax.rem(self.y + (1 if direction == 0 else NY - 1), NY)}

    def hop(self, direction, k):
        src = self.own if k == 1 else self.slot(direction, k - 1, self.c)
        dst = self.slot(direction, k - 1, self.c)
        copy = remote(src, dst, self.send.at[direction, k], self.recv.at[direction, k], self.neighbour(direction))
        copy.start()
        self.started.append(copy)

    def to_partner(self, src, dst, index):
        copy = remote(src, dst, self.psend.at[index], self.precv.at[index], {"c": 1 - self.c})
        copy.start()
        self.started.append(copy)

    def begin(self):
        self.hop(0, 1)
        self.hop(1, 1)
        mine = self.slot(0, 0, self.c)
        self.to_partner(self.own, mine, 0)
        pltpu.sync_copy(self.own, mine)

    def step(self, k):
        for direction, last in ((0, HALF_Y), (1, HALF_Y - 1)):
            if k <= last:
                here = self.slot(direction, k, self.c)
                remote(
                    here, here, self.send.at[direction, k], self.recv.at[direction, k], self.neighbour(direction)
                ).wait_recv()
                if k < last:
                    self.hop(direction, k + 1)
                self.to_partner(here, here, k + (HALF_Y if direction else 0))

    def finish(self):
        for direction, last in ((0, HALF_Y), (1, HALF_Y - 1)):
            for k in range(0 if direction == 0 else 1, last + 1):
                index = k + (HALF_Y if direction else 0)
                there = self.slot(direction, k, 1 - self.c)
                remote(
                    there, there, self.psend.at[index], self.precv.at[index], {"c": 1 - self.c}
                ).wait_recv()
        for copy in self.started:
            copy.wait_send()


def gather_kernel(
    sel_ref,
    pairs_ref,
    text_ref,
    cot_ref,
    wo_ref,
    kv_ref,
    text_all,
    cot_all,
    wo_all,
    picked,
    zsend,
    zrecv,
    xsend,
    xrecv,
    tsend,
    trecv,
    tpsend,
    tprecv,
    csend,
    crecv,
    cpsend,
    cprecv,
    wsend,
    wrecv,
    *slots,
):
    z, x, y, c = position()
    me = 2 * y + c
    fsdp = fsdp_peers(y, c)
    ups = ({"z": lax.rem(z + 1, NZ)}, {"z": lax.rem(z + NZ - 1, NZ)})
    meet([*ups, *x_peers(x), *fsdp])()

    held = ([pairs_ref, *slots[:HALF_Z]], [pairs_ref, *slots[HALF_Z:]] + [slots[HALF_Z - 1]])

    def exists(direction, k, ch):
        return k < HALF_Z or (k == HALF_Z and (ch == CHUNKS - 1) == (direction == 1))

    def zcopy(direction, k, ch):
        rows = pl.ds(ch * CHUNK_ROWS, CHUNK_ROWS)
        return remote(
            held[direction][k - 1].at[rows],
            held[direction][k].at[rows],
            zsend.at[direction, k, ch],
            zrecv.at[direction, k, ch],
            ups[direction],
        )

    zcopies = {
        (d, k, ch): zcopy(d, k, ch)
        for k in range(1, HALF_Z + 1)
        for ch in range(CHUNKS)
        for d in range(2)
        if exists(d, k, ch)
    }
    for ch in range(CHUNKS):
        for d in range(2):
            zcopies[d, 1, ch].start()

    text_ring = YRing(text_ref, text_all, y, c, tsend, trecv, tpsend, tprecv)
    cot_ring = YRing(cot_ref, cot_all, y, c, csend, crecv, cpsend, cprecv)
    text_ring.begin()

    xcopies = []

    def deliver(block, kk):
        for dx in range(NX):
            wanted = sel_ref[kk * NX + dx]
            image = block[:LAT, :]
            for i in range(1, IMG):
                image = jnp.where(wanted == i, block[i * LAT : (i + 1) * LAT, :], image)
            if dx == 0:
                kv_ref[kk] = image
            else:
                picked[dx - 1, kk] = image
                copy = remote(
                    picked.at[dx - 1, kk],
                    kv_ref.at[dx * NZ + kk],
                    xsend.at[dx - 1, kk],
                    xrecv.at[dx - 1, kk],
                    {"x": lax.rem(x + dx, NX)},
                )
                copy.start()
                xcopies.append(copy)

    deliver(pairs_ref, 0)

    wcopies = []

    def send_weight(index):
        if index == 0:
            core, row = 1 - c, y
        else:
            row = lax.rem(y + (index + 1) // 2, NY)
            core = lax.rem(c + (index + 1) % 2, 2)
        columns = pl.ds(pl.multiple_of((2 * row + core) * 256, 256), 256)
        copy = remote(
            wo_ref.at[:, columns], wo_all.at[me], wsend.at[index], wrecv.at[index], {"y": row, "c": core}
        )
        copy.start()
        wcopies.append(copy)

    def own_weight():
        wo_all[me] = wo_ref[:, pl.ds(pl.multiple_of(me * 256, 256), 256)]

    todo = {}
    for k in range(1, HALF_Y + 1):
        todo.setdefault(2 * k - 1, []).append(functools.partial(text_ring.step, k))
        todo.setdefault(2 * k + 7, []).append(functools.partial(cot_ring.step, k))
    todo.setdefault(6, []).append(cot_ring.begin)
    todo.setdefault(6, []).append(own_weight)
    order = [7, 8, 9, 5, 6, 10, 3, 4, 11, 12, 1, 2, 13, 14, 0]
    for at, index in enumerate(order):
        todo.setdefault(4 + at // 2, []).append(functools.partial(send_weight, index))

    turn = 0
    for k in range(1, HALF_Z + 1):
        for ch in range(CHUNKS):
            for d in range(2):
                if exists(d, k, ch):
                    zcopies[d, k, ch].wait_recv()
                    if (d, k + 1, ch) in zcopies:
                        zcopies[d, k + 1, ch].start()
            for action in todo.get(turn, ()):
                action()
            turn += 1
        deliver(held[0][k], k)
        if k < HALF_Z:
            deliver(held[1][k], NZ - k)

    text_ring.finish()
    cot_ring.finish()
    for index in range(GROUP - 1):
        if index == 0:
            core, row = 1 - c, y
        else:
            row = lax.rem(y + NY - (index + 1) // 2, NY)
            core = lax.rem(c + (index + 1) % 2, 2)
        there = wo_all.at[2 * row + core]
        remote(there, there, wsend.at[index], wrecv.at[index], {"y": row, "c": core}).wait_recv()
    for copy in xcopies:
        copy.wait_recv()
    for copy in [*zcopies.values(), *xcopies, *wcopies]:
        copy.wait_send()


def gather_call(sel, pairs, text, cot, wo):
    vmem = pl.BlockSpec(memory_space=pltpu.VMEM)
    dma = pltpu.SemaphoreType.DMA
    ring = [dma((2, HALF_Y + 1)), dma((2, HALF_Y + 1)), dma((NY,)), dma((NY,))]
    return pl.pallas_call(
        gather_kernel,
        out_shape=(
            jax.ShapeDtypeStruct((NX * NZ, LAT, 256), BF16),
            jax.ShapeDtypeStruct((GROUP, TOK, 256), BF16),
            jax.ShapeDtypeStruct((GROUP, TOK, 256), BF16),
            jax.ShapeDtypeStruct((GROUP, 128, 256), BF16),
        ),
        in_specs=[pl.BlockSpec(memory_space=pltpu.SMEM)] + [vmem] * 4,
        out_specs=(vmem,) * 4,
        scratch_shapes=[
            pltpu.VMEM((NX - 1, NZ, LAT, 256), BF16),
            dma((2, HALF_Z + 1, CHUNKS)),
            dma((2, HALF_Z + 1, CHUNKS)),
            dma((NX - 1, NZ)),
            dma((NX - 1, NZ)),
            *ring,
            *ring,
            dma((GROUP - 1,)),
            dma((GROUP - 1,)),
        ]
        + [pltpu.VMEM((IMG * LAT, 256), BF16)] * (NZ - 1),
        compiler_params=pltpu.CompilerParams(
            collective_id=0, has_side_effects=True, vmem_limit_bytes=20 << 20
        ),
        name="gather_inputs",
    )(sel, pairs, text, cot, wo)


def attend_kernel(index_ref, text_all, wq_ref, gain_ref, bias_ref, kv_ref, pos_ref, ctx_ref):
    width = GROUP * 256
    total = jnp.zeros((TOK, 128), F32)
    for f in range(GROUP):
        block = text_all[f].astype(F32)
        total = total + block[:, :128] + block[:, 128:]
    mean = jnp.sum(total, axis=-1, keepdims=True) / width
    total = jnp.zeros((TOK, 128), F32)
    for f in range(GROUP):
        centered = text_all[f].astype(F32) - mean
        squared = centered * centered
        total = total + squared[:, :128] + squared[:, 128:]
    scale = lax.rsqrt(jnp.sum(total, axis=-1, keepdims=True) / width + EPSILON)
    acc = jnp.zeros((TOK, 128), F32)
    for f in range(GROUP):
        centered = text_all[f].astype(F32) - mean
        normed = (centered * scale * gain_ref[f : f + 1, :] + bias_ref[f : f + 1, :]).astype(BF16)
        acc = acc + jnp.dot(normed, wq_ref[f * 256 : (f + 1) * 256, :], preferred_element_type=F32)
    queries = (acc * 128 ** (-0.5)).astype(BF16)
    for s in range(3):
        rows = slice(s * LAT, (s + 1) * LAT)
        blocks = [kv_ref[index_ref[s * 5 + k]] for k in range(5)]
        keys = jnp.concatenate([b[:, :128] for b in blocks], axis=0)
        values = jnp.concatenate([b[:, 128:] for b in blocks], axis=0)
        scores = lax.dot_general(queries[rows], keys, (((1,), (1,)), ((), ())), preferred_element_type=F32)
        pos = pos_ref[rows, :]
        column = lax.broadcasted_iota(jnp.int32, scores.shape, 1) // LAT
        scores = jnp.where(pos == column, scores, -1e30)
        weights = jnp.exp(scores - jnp.max(scores, axis=-1, keepdims=True))
        probs = (weights / jnp.sum(weights, axis=-1, keepdims=True)).astype(BF16)
        context = jnp.dot(probs, values, preferred_element_type=F32)
        ctx_ref[rows, :] = jnp.where(pos >= 0, context, 0.0).astype(BF16)


def attend_call(index, text_all, wq, gain, bias, kv, pos):
    vmem = pl.BlockSpec(memory_space=pltpu.VMEM)
    return pl.pallas_call(
        attend_kernel,
        out_shape=jax.ShapeDtypeStruct((TOK, 128), BF16),
        in_specs=[pl.BlockSpec(memory_space=pltpu.SMEM)] + [vmem] * 6,
        out_specs=vmem,
        compiler_params=pltpu.CompilerParams(vmem_limit_bytes=16 << 20),
        name="attend",
    )(index, text_all, wq, gain, bias, kv, pos)


FAR_FIRST = [8, 7, 9, 6, 10, 5, 11, 4, 12, 3, 13, 2, 14, 1, 15, 0]


def combine_kernel(
    gate_ref,
    ctx_ref,
    cot_all,
    wo_all,
    text_ref,
    out_ref,
    grad_ref,
    product,
    own,
    gsend,
    grecv,
    hsend,
    hrecv,
    same,
    other,
    xs,
    xr,
    zs,
    zr,
    ys,
    yr,
    ps,
    pr,
):
    z, x, y, c = position()
    zpeers = [{"z": lax.rem(z + kk, NZ)} for kk in range(NZ)]
    xpeers = x_peers(x)
    ypeers = [{"y": lax.rem(y + dy, NY)} for dy in range(NY)]
    partner = {"c": 1 - c}
    meet([*zpeers[1:], *xpeers, *ypeers[1:], partner])()
    started = []

    def go(copy):
        copy.start()
        started.append(copy)
        return copy

    ycopies = {}
    for dy in (4, 3, 5, 2, 6, 1, 7):
        ycopies[dy] = go(remote(ctx_ref, same.at[dy], ys.at[dy], yr.at[dy], ypeers[dy]))
    pcopies = {0: go(remote(ctx_ref, other.at[0], ps.at[0], pr.at[0], partner))}

    context = ctx_ref[...]
    xcopies = {}
    for kk in FAR_FIRST:
        block = cot_all[lax.rem(z + kk, NZ)]
        product[kk] = lax.dot_general(block, context, (((0,), (0,)), ((), ())), preferred_element_type=F32)
        for dx in range(NX):
            rows = pl.ds(pl.multiple_of(lax.rem(x + dx, NX) * 64, 64), 64)
            part = product[kk, rows, :]
            if dx == 0:
                own[kk] = part
            else:
                gsend[dx - 1, kk] = part.astype(BF16)
                xcopies[dx, kk] = go(
                    remote(
                        gsend.at[dx - 1, kk],
                        grecv.at[dx - 1, kk],
                        xs.at[dx - 1, kk],
                        xr.at[dx - 1, kk],
                        xpeers[dx - 1],
                    )
                )
    def pass_on(dy):
        ycopies[dy].wait_recv()
        pcopies[dy] = go(remote(same.at[dy], other.at[dy], ps.at[dy], pr.at[dy], partner))

    near = [1, 7, 2, 6, 3, 5, 4]
    zcopies = {}
    for at, kk in enumerate(FAR_FIRST):
        total = own[kk]
        for dx in range(1, NX):
            xcopies[dx, kk].wait_recv()
            total = total + grecv[dx - 1, kk].astype(F32)
        if kk == 0:
            own[0] = total
        else:
            hsend[kk] = total.astype(BF16)
            zcopies[kk] = go(remote(hsend.at[kk], hrecv.at[kk], zs.at[kk], zr.at[kk], zpeers[kk]))
        if at % 2 == 1 and near:
            pass_on(near.pop(0))
    gate = gate_ref[0]
    update = jnp.zeros((TOK, 256), F32)
    for dy in (0, 1, 7, 2, 6, 3, 5, 4):
        row = 2 * lax.rem(y + NY - dy, NY)
        mine = context if dy == 0 else same[dy]
        update = update + jnp.dot(mine, wo_all[row + c], preferred_element_type=F32)
        pcopies[dy].wait_recv()
        update = update + jnp.dot(other[dy], wo_all[row + 1 - c], preferred_element_type=F32)
    out_ref[...] = (text_ref[...].astype(F32) + gate * update).astype(BF16)
    total = own[0]
    for kk in FAR_FIRST[::-1][1:]:
        zcopies[kk].wait_recv()
        total = total + hrecv[kk].astype(F32)
    grad_ref[...] = jnp.transpose(gate * total, (1, 0))
    for copy in started:
        copy.wait_send()


def combine_call(gate, ctx, cot_all, wo_all, text):
    vmem = pl.BlockSpec(memory_space=pltpu.VMEM)
    dma = pltpu.SemaphoreType.DMA
    return pl.pallas_call(
        combine_kernel,
        out_shape=(jax.ShapeDtypeStruct((TOK, 256), BF16), jax.ShapeDtypeStruct((128, 64), F32)),
        in_specs=[pl.BlockSpec(memory_space=pltpu.SMEM)] + [vmem] * 4,
        out_specs=(vmem, vmem),
        scratch_shapes=[
            pltpu.VMEM((NZ, 256, 128), F32),
            pltpu.VMEM((NZ, 64, 128), F32),
            pltpu.VMEM((NX - 1, NZ, 64, 128), BF16),
            pltpu.VMEM((NX - 1, NZ, 64, 128), BF16),
            pltpu.VMEM((NZ, 64, 128), BF16),
            pltpu.VMEM((NZ, 64, 128), BF16),
            pltpu.VMEM((NY, TOK, 128), BF16),
            pltpu.VMEM((NY, TOK, 128), BF16),
            dma((NX - 1, NZ)),
            dma((NX - 1, NZ)),
            dma((NZ,)),
            dma((NZ,)),
            dma((NY,)),
            dma((NY,)),
            dma((NY,)),
            dma((NY,)),
        ],
        compiler_params=pltpu.CompilerParams(
            collective_id=1, has_side_effects=True, vmem_limit_bytes=16 << 20
        ),
        name="combine_outputs",
    )(gate, ctx, cot_all, wo_all, text)


def routes(media_refs, owner_map, z, x):
    refs = lax.dynamic_slice_in_dim(media_refs.reshape(NZ, NX * 15), z, 1, 0).reshape(NX * 15)
    lookup = jnp.maximum(refs, 0)[:, None] == jnp.arange(owner_map.shape[0], dtype=jnp.int32)
    storage = jnp.sum(jnp.where(lookup, owner_map, 0), axis=-1)
    owner, within = storage // IMG, storage % IMG
    dz = (z + NZ - owner // NX) % NZ
    source_x = owner % NX
    dest_dx = (jnp.arange(NX * 15, dtype=jnp.int32) // 15 + NX - x) % NX
    cell = jnp.arange(NZ * NX, dtype=jnp.int32)[:, None]
    hit = (refs >= 0) & (source_x == x) & (dz * NX + dest_dx == cell)
    sel = jnp.sum(jnp.where(hit, within, 0), axis=-1)
    index = ((x + NX - source_x) % NX) * NZ + dz
    index = lax.dynamic_slice_in_dim(index, x * 15, 15, 0)
    return sel, index


def body(
    text_states,
    cotangent,
    norm_gain,
    norm_bias,
    branch_gate,
    query_weight,
    latent_weight,
    output_weight,
    latents,
    media_refs,
    media_pos,
    owner_map,
):
    z, x = lax.axis_index("z"), lax.axis_index("x")
    pairs = jnp.dot(
        latents.reshape(IMG * LAT, -1), latent_weight.reshape(-1, 256), preferred_element_type=F32
    ).astype(BF16)
    sel, index = routes(media_refs, owner_map, z, x)
    text = text_states.reshape(TOK, 256)
    kv, text_all, cot_all, wo_all = gather_call(
        sel, pairs, text, cotangent.reshape(TOK, 256), output_weight.reshape(128, -1)
    )
    context = attend_call(
        index,
        text_all,
        query_weight.reshape(-1, 128),
        norm_gain.reshape(GROUP, 256),
        norm_bias.reshape(GROUP, 256),
        kv,
        media_pos.reshape(TOK, 1),
    )
    layer_out, out_grad = combine_call(jnp.tanh(branch_gate), context, cot_all, wo_all, text)
    return layer_out.reshape(3, 64, 256), out_grad.reshape(1, 128, 64)


def solution(mesh):
    split = Mesh(mesh.devices.reshape(NZ, NX, NY, 2), ("z", "x", "y", "c"))
    dp, fsdp = ("z", "x"), ("y", "c")
    return jax.shard_map(
        body,
        mesh=split,
        in_specs=(
            P(dp, None, fsdp),
            P(dp, None, fsdp),
            P(),
            P(),
            P(),
            P(None, fsdp, None),
            P(None, fsdp, None),
            P(fsdp, None, None),
            P(dp, None, None),
            P(),
            P(dp, None),
            P(),
        ),
        out_specs=(P(dp, None, fsdp), P(fsdp, None, dp)),
        check_vma=False,
    )
```

time: 344 us -> 136 us (0.40)
  the two profiles are of different devices: /device:TPU:6 before, /device:TPU:8 now
where the time goes in v1:
time: 136 us
  Pallas kernels  119 us (88%)
  local copies, waits for them, and re-layouts  10.2 us (7%)
  matrix products  3.8 us (3%)
  between operations  1.72 us (1%)
    pallas_call x1, Pallas kernels, gather_call(): pl.pallas_call(gather_kernel, out_shape=(jax.ShapeDtypeStruct((NX * NZ, L...  90.4 us
    pallas_call x1, Pallas kernels, combine_call(): pl.pallas_call(combine_kernel, out_shape=(jax.ShapeDtypeStruct((TOK, 256)...  25.7 us
    unnamed x35, local copies, waits for them, and re-layouts  9.87 us
    dot_general x1, matrix products, body(): jnp.dot(latents.reshape(IMG * LAT, -1), latent_weight.reshape(-1, 256), p...  3.8 us
    pallas_call x1, Pallas kernels, attend_call(): pl.pallas_call(attend_kernel, out_shape=jax.ShapeDtypeStruct((TOK, 128),...  2.95 us

profile of v1, /device:TPU:8, one launch (start us, length us, event | category | flops | bytes accessed | tf_op | source)
XLA Modules:
  0.0 135.8 jit_solution(9116222060181393203)
XLA Ops:
  0.6 0.0 copy-start
  1.5 0.8 copy.19
  2.3 0.1 reshape.179
  2.4 0.9 select_reduce_fusion
  3.4 0.1 dynamic_slice.7.index_ref
  3.5 0.1 select_reduce_fusion.1.sel_ref
  3.6 0.0 copy-done
  3.6 0.0 copy-start.8
  3.6 0.0 copy-start.11
  3.6 0.0 copy-start.12
  3.6 0.0 copy-start.13
  3.6 0.0 copy-start.14
  3.7 0.0 copy-start.15
  3.7 3.8 %fusion.2.pairs_ref = bf16[576,256]{1,0:T(8,128)(2,1)S(1)} fusion(bf16[576,4096]{1,0:T(8,128)(2,1)} %bitcast.30, bf16[4096,1,256]{2,0,1:T(8,128)(2,1)S(1)} %copy-done), kind=kOutput, calls=%fused_computation.2 | convolution fusion | flops 1208107008 | bytes 7110656 | tf_op jit(solution)/shard_map/dot_general | solution.py:502
  7.5 0.0 copy-start.7
  7.5 0.0 copy-done.8
  7.5 0.0 copy-done.11
  7.5 0.0 copy-done.12
  7.5 90.4 %gather_inputs.1 = (bf16[64,64,256]{2,1,0:T(8,128)(2,1)S(1)}, bf16[16,192,256]{2,1,0:T(8,128)(2,1)S(1)}, bf16[16,192,256]{2,1,0:T(8,128)(2,1)S(1)}, bf16[16,128,256]{2,1,0:T(8,128)(2,1)S(1)}) custom-call(s32[64]{0:T(128)S(1)} %select_reduce_fusion.1.sel_ref, bf16[576,256]{1,0:T(8,128)(2,1)S(1)} %fusion.2.pairs_ref, bf16[192,256]{1,0:T(8,128)(2,1)S(1)} %bitcast.25, ...), custom_call_target="tpu_custom_call" | custom-call | tf_op jit(solution)/shard_map/gather_inputs/pallas_call | solution.py:260
  97.9 1.3 copy-done.1
  99.2 1.2 copy-done.3
  100.4 1.2 copy-done.5
  101.6 1.0 copy-done.9
  102.6 0.1 reshape.191.pos_ref
  102.8 0.0 copy-done.7
  102.8 0.0 copy-start.2
  102.8 1.6 %copy-done.2 = bf16[64,64,256]{2,1,0:T(8,128)(2,1)S(1)} copy-done((bf16[64,64,256]{2,1,0:T(8,128)(2,1)S(1)}, bf16[64,64,256]{2,1,0:T(8,128)(2,1)}, u32[]{:S(2)}) %copy-start.2) | copy-done | bytes 2097176
  104.4 1.4 %copy-done.4 = bf16[16,192,256]{2,1,0:T(8,128)(2,1)S(1)} copy-done((bf16[16,192,256]{2,1,0:T(8,128)(2,1)S(1)}, bf16[16,192,256]{2,1,0:T(8,128)(2,1)}, u32[]{:S(2)}) %copy-start.4) | copy-done | bytes 1572888
  105.8 3.0 %attend.1.ctx_ref = bf16[192,128]{1,0:T(8,128)(2,1)S(1)} custom-call(s32[15]{0:T(128)S(1)} %dynamic_slice.7.index_ref, bf16[16,192,256]{2,1,0:T(8,128)(2,1)S(1)} %copy-done.4, bf16[4096,128]{1,0:T(8,128)(2,1)S(1)} %bitcast.23, f32[16,256]{1,0:T(8,128)S(1)} %reshape.186.gain_ref, f32[16,256]{1,0:T(8,128)S(1)} %reshape.187.bias_ref, ...), custom_call_target="tpu_custom_call" | custom-call | tf_op jit(solution)/shard_map/attend/pallas_call | solution.py:325
  108.8 25.7 %combine_outputs.1 = (bf16[192,256]{1,0:T(8,128)(2,1)S(1)}, f32[128,64]{1,0:T(8,128)S(1)}) custom-call(f32[1]{0:T(128)S(6)} %tanh.3.gate_ref, bf16[192,128]{1,0:T(8,128)(2,1)S(1)} %attend.1.ctx_ref, bf16[16,192,256]{2,1,0:T(8,128)(2,1)S(1)} %copy-done.6, bf16[16,128,256]{2,1,0:T(8,128)(2,1)S(1)} %copy-done.10, bf16[192,256]{1,0:T(8,128)(2,1)S(1)} %bitcast.26), custom_call_target="tpu_custom_call" | custom-call | tf_op jit(solution)/shard_map/combine_outputs/pallas_call | solution.py:441
  134.5 0.7 copy.21
  135.2 0.6 copy.24
  (18 shorter events, 0.1 us)
Async XLA Ops:
  0.6 3.0 %copy-start = (bf16[4096,1,256]{2,0,1:T(8,128)(2,1)S(1)}, bf16[4096,1,256]{2,0,1:T(8,128)(2,1)}, u32[]{:S(2)}) copy-start(bf16[4096,1,256]{2,0,1:T(8,128)(2,1)} %param.18) | copy-start | bytes 6291460
  3.6 3.9 %copy-start.8 = (bf16[1,128,4096]{2,1,0:T(8,128)(2,1)S(1)}, bf16[1,128,4096]{2,1,0:T(8,128)(2,1)}, u32[]{:S(2)}) copy-start(bf16[1,128,4096]{2,1,0:T(8,128)(2,1)} %param.19) | copy-start | bytes 3145732
  3.6 3.9 %copy-start.11 = (bf16[3,64,256]{2,1,0:T(8,128)(2,1)S(1)}, bf16[3,64,256]{2,1,0:T(8,128)(2,1)}, u32[]{:S(2)}) copy-start(bf16[3,64,256]{2,1,0:T(8,128)(2,1)} %param.12) | copy-start | bytes 294916
  3.6 3.9 %copy-start.12 = (bf16[3,64,256]{2,1,0:T(8,128)(2,1)S(1)}, bf16[3,64,256]{2,1,0:T(8,128)(2,1)}, u32[]{:S(2)}) copy-start(bf16[3,64,256]{2,1,0:T(8,128)(2,1)} %param.13) | copy-start | bytes 294916
  3.6 99.0 %copy-start.13 = (f32[4096]{0:T(1024)S(1)}, f32[4096]{0:T(1024)}, u32[]{:S(2)}) copy-start(f32[4096]{0:T(1024)} %param.14) | copy-start | bytes 49156
  3.6 99.0 %copy-start.14 = (f32[4096]{0:T(1024)S(1)}, f32[4096]{0:T(1024)}, u32[]{:S(2)}) copy-start(f32[4096]{0:T(1024)} %param.15) | copy-start | bytes 49156
  3.7 99.0 %copy-start.15 = (s32[3,64]{1,0:T(4,128)S(1)}, s32[3,64]{1,0:T(4,128)}, u32[]{:S(2)}) copy-start(s32[3,64]{1,0:T(4,128)} %param.22) | copy-start | bytes 2308
  7.5 95.3 %copy-start.7 = (bf16[4096,1,128]{2,0,1:T(8,128)(2,1)S(1)}, bf16[4096,1,128]{2,0,1:T(8,128)(2,1)}, u32[]{:S(2)}) copy-start(bf16[4096,1,128]{2,0,1:T(8,128)(2,1)} %param.17) | copy-start | bytes 3145732
  97.9 1.3 copy-start.1
  99.2 1.2 copy-start.3
  100.4 1.2 copy-start.5
  101.6 1.0 copy-start.9
  102.8 1.6 %copy-start.2 = (bf16[64,64,256]{2,1,0:T(8,128)(2,1)S(1)}, bf16[64,64,256]{2,1,0:T(8,128)(2,1)}, u32[]{:S(2)}) copy-start(bf16[64,64,256]{2,1,0:T(8,128)(2,1)} %copy-done.1) | copy-start | bytes 6291460
  104.4 1.4 %copy-start.4 = (bf16[16,192,256]{2,1,0:T(8,128)(2,1)S(1)}, bf16[16,192,256]{2,1,0:T(8,128)(2,1)}, u32[]{:S(2)}) copy-start(bf16[16,192,256]{2,1,0:T(8,128)(2,1)} %copy-done.3) | copy-start | bytes 4718596
  105.8 3.0 %copy-start.6 = (bf16[16,192,256]{2,1,0:T(8,128)(2,1)S(1)}, bf16[16,192,256]{2,1,0:T(8,128)(2,1)}, u32[]{:S(2)}) copy-start(bf16[16,192,256]{2,1,0:T(8,128)(2,1)} %copy-done.5) | copy-start | bytes 4718596
  105.8 3.0 %copy-start.10 = (bf16[16,128,256]{2,1,0:T(8,128)(2,1)S(1)}, bf16[16,128,256]{2,1,0:T(8,128)(2,1)}, u32[]{:S(2)}) copy-start(bf16[16,128,256]{2,1,0:T(8,128)(2,1)} %copy-done.9) | copy-start | bytes 3145732

commit v2 on v1

v2 whole, which is shorter than its diff:
```python
import functools

import jax
import jax.numpy as jnp
from jax import lax
from jax.experimental import pallas as pl
from jax.experimental.pallas import tpu as pltpu
from jax.sharding import Mesh
from jax.sharding import PartitionSpec as P

EPSILON = 1e-05
MESH = pl.DeviceIdType.MESH
NZ, NX, NY = 16, 4, 8
GROUP = 2 * NY
IMG = 9
LAT = 64
TOK = 192
CHUNKS = 3
CHUNK_ROWS = IMG * LAT // CHUNKS
QUARTER = 128 // NX
HALF_Z = NZ // 2
HALF_Y = NY // 2
BF16 = jnp.bfloat16
F32 = jnp.float32


def remote(src, dst, send, recv, where):
    return pltpu.make_async_remote_copy(
        src_ref=src, dst_ref=dst, send_sem=send, recv_sem=recv, device_id=where, device_id_type=MESH
    )


def position():
    return lax.axis_index("z"), lax.axis_index("x"), lax.axis_index("y"), lax.axis_index("c")


def meet(targets):
    barrier = pltpu.get_barrier_semaphore()
    for where in targets:
        pl.semaphore_signal(barrier, inc=1, device_id=where, device_id_type=MESH)
    return lambda: pl.semaphore_wait(barrier, len(targets))


def fsdp_peers(y, c):
    peers = [{"c": 1 - c}]
    for dy in range(1, NY):
        for dc in range(2):
            peers.append({"y": lax.rem(y + dy, NY), "c": lax.rem(c + dc, 2)})
    return peers


def x_peers(x):
    return [{"x": lax.rem(x + dx, NX)} for dx in range(1, NX)]


class YRing:
    def __init__(self, own, full, y, c, send, recv, psend, precv):
        self.own, self.full, self.y, self.c = own, full, y, c
        self.send, self.recv, self.psend, self.precv = send, recv, psend, precv
        self.started = []

    def slot(self, direction, k, core):
        row = lax.rem(self.y + (NY - k if direction == 0 else k), NY)
        return self.full.at[2 * row + core]

    def neighbour(self, direction):
        return {"y": lax.rem(self.y + (1 if direction == 0 else NY - 1), NY)}

    def hop(self, direction, k):
        src = self.own if k == 1 else self.slot(direction, k - 1, self.c)
        dst = self.slot(direction, k - 1, self.c)
        copy = remote(src, dst, self.send.at[direction, k], self.recv.at[direction, k], self.neighbour(direction))
        copy.start()
        self.started.append(copy)

    def to_partner(self, src, dst, index):
        copy = remote(src, dst, self.psend.at[index], self.precv.at[index], {"c": 1 - self.c})
        copy.start()
        self.started.append(copy)

    def begin(self):
        self.hop(0, 1)
        self.hop(1, 1)
        mine = self.slot(0, 0, self.c)
        self.to_partner(self.own, mine, 0)
        self.local = pltpu.make_async_copy(self.own, mine, self.psend.at[NY])
        self.local.start()

    def step(self, k):
        for direction, last in ((0, HALF_Y), (1, HALF_Y - 1)):
            if k <= last:
                here = self.slot(direction, k, self.c)
                remote(
                    here, here, self.send.at[direction, k], self.recv.at[direction, k], self.neighbour(direction)
                ).wait_recv()
                if k < last:
                    self.hop(direction, k + 1)
                self.to_partner(here, here, k + (HALF_Y if direction else 0))

    def finish(self):
        self.local.wait()
        for direction, last in ((0, HALF_Y), (1, HALF_Y - 1)):
            for k in range(0 if direction == 0 else 1, last + 1):
                index = k + (HALF_Y if direction else 0)
                there = self.slot(direction, k, 1 - self.c)
                remote(
                    there, there, self.psend.at[index], self.precv.at[index], {"c": 1 - self.c}
                ).wait_recv()
        for copy in self.started:
            copy.wait_send()


FAR_FIRST = [8, 7, 9, 6, 10, 5, 11, 4, 12, 3, 13, 2, 14, 1, 15, 0]


def fused_kernel(
    sel_ref,
    index_ref,
    gate_ref,
    latents_ref,
    wl_hbm,
    text_ref,
    cot_ref,
    wo_ref,
    wq_hbm,
    gain_ref,
    bias_ref,
    pos_ref,
    out_ref,
    grad_ref,
    wl_ref,
    wq_ref,
    lat,
    pairs_ref,
    kv_ref,
    text_all,
    cot_all,
    wo_all,
    picked,
    ctx_ref,
    product,
    own,
    gsend,
    grecv,
    hsend,
    hrecv,
    same,
    other,
    lsem,
    zsend,
    zrecv,
    xsend,
    xrecv,
    tsend,
    trecv,
    tpsend,
    tprecv,
    csend,
    crecv,
    cpsend,
    cprecv,
    wsend,
    wrecv,
    wxs,
    wxr,
    xs,
    xr,
    zs,
    zr,
    ys,
    yr,
    ps,
    pr,
    *slots,
):
    z, x, y, c = position()
    me = 2 * y + c
    ups = ({"z": lax.rem(z + 1, NZ)}, {"z": lax.rem(z + NZ - 1, NZ)})

    def chunk_rows(ch):
        return pl.ds(ch * CHUNK_ROWS, CHUNK_ROWS)

    loads = [
        pltpu.make_async_copy(latents_ref.at[chunk_rows(ch)], lat.at[chunk_rows(ch)], lsem.at[ch])
        for ch in range(CHUNKS)
    ]
    weight_load = pltpu.make_async_copy(wl_hbm, wl_ref, lsem.at[CHUNKS])
    query_load = pltpu.make_async_copy(wq_hbm, wq_ref, lsem.at[CHUNKS + 1])
    weight_load.start()
    for load in [*loads, query_load]:
        load.start()
    wait_peers = meet([*ups, *x_peers(x), *fsdp_peers(y, c)])
    started = []

    def go(copy):
        copy.start()
        started.append(copy)
        return copy

    held = ([pairs_ref, *slots[:HALF_Z]], [pairs_ref, *slots[HALF_Z:]] + [slots[HALF_Z - 1]])

    def exists(direction, k, ch):
        return k < HALF_Z or (k == HALF_Z and (ch == CHUNKS - 1) == (direction == 1))

    def zcopy(direction, k, ch):
        return remote(
            held[direction][k - 1].at[chunk_rows(ch)],
            held[direction][k].at[chunk_rows(ch)],
            zsend.at[direction, k, ch],
            zrecv.at[direction, k, ch],
            ups[direction],
        )

    zcopies = {}

    def hop(direction, k, ch):
        zcopies[direction, k, ch] = go(zcopy(direction, k, ch))

    text_ring = YRing(text_ref, text_all, y, c, tsend, trecv, tpsend, tprecv)
    cot_ring = YRing(cot_ref, cot_all, y, c, csend, crecv, cpsend, cprecv)

    weight_load.wait()
    for ch in range(CHUNKS):
        loads[ch].wait()
        pairs_ref[chunk_rows(ch), :] = jnp.dot(
            lat[chunk_rows(ch), :], wl_ref[...], preferred_element_type=F32
        ).astype(BF16)
        if ch == 0:
            wait_peers()
            text_ring.begin()
        for d in range(2):
            hop(d, 1, ch)

    xcopies = []

    def deliver(block, kk):
        for dx in (1, 2, 3, 0):
            wanted = sel_ref[kk * NX + dx]
            image = block[:LAT, :]
            for i in range(1, IMG):
                image = jnp.where(wanted == i, block[i * LAT : (i + 1) * LAT, :], image)
            if dx == 0:
                kv_ref[kk] = image
            else:
                picked[dx - 1, kk] = image
                xcopies.append(
                    go(
                        remote(
                            picked.at[dx - 1, kk],
                            kv_ref.at[dx * NZ + kk],
                            xsend.at[dx - 1, kk],
                            xrecv.at[dx - 1, kk],
                            {"x": lax.rem(x + dx, NX)},
                        )
                    )
                )

    def fsdp_place(index, sign):
        if index == 0:
            return y, 1 - c
        step = (index + 1) // 2
        row = lax.rem(y + (step if sign > 0 else NY - step), NY)
        return row, lax.rem(c + (index + 1) % 2, 2)

    quarter = pl.ds(pl.multiple_of(x * QUARTER, QUARTER), QUARTER)

    def weight_columns(row, core):
        return pl.ds(pl.multiple_of((2 * row + core) * 256, 256), 256)

    own_weight = pltpu.make_async_copy(
        wo_ref.at[quarter, weight_columns(y, c)], wo_all.at[me, quarter], lsem.at[CHUNKS + 2]
    )

    def send_weight(index):
        row, core = fsdp_place(index, 1)
        go(
            remote(
                wo_ref.at[quarter, weight_columns(row, core)],
                wo_all.at[me, quarter],
                wsend.at[index],
                wrecv.at[index],
                {"y": row, "c": core},
            )
        )

    def spread_weight():
        own_weight.wait()
        for index in range(GROUP - 1):
            row, core = fsdp_place(index, -1)
            there = wo_all.at[2 * row + core, quarter]
            remote(there, there, wsend.at[index], wrecv.at[index], {"y": row, "c": core}).wait_recv()
        for dx in range(1, NX):
            mine = wo_all.at[:, quarter]
            go(remote(mine, mine, wxs.at[dx], wxr.at[dx], {"x": lax.rem(x + dx, NX)}))

    def weight_spread():
        for dx in range(1, NX):
            rows = pl.ds(pl.multiple_of(lax.rem(x + NX - dx, NX) * QUARTER, QUARTER), QUARTER)
            there = wo_all.at[:, rows]
            remote(there, there, wxs.at[dx], wxr.at[dx], {"x": lax.rem(x + dx, NX)}).wait_recv()

    state = {}
    width = GROUP * 256

    def norm_mean():
        text_ring.finish()
        total = jnp.zeros((TOK, 128), F32)
        for f in range(GROUP):
            block = text_all[f].astype(F32)
            total = total + block[:, :128] + block[:, 128:]
        state["mean"] = jnp.sum(total, axis=-1, keepdims=True) / width

    def norm_scale():
        total = jnp.zeros((TOK, 128), F32)
        for f in range(GROUP):
            centered = text_all[f].astype(F32) - state["mean"]
            squared = centered * centered
            total = total + squared[:, :128] + squared[:, 128:]
        state["scale"] = lax.rsqrt(jnp.sum(total, axis=-1, keepdims=True) / width + EPSILON)

    def project(first, last):
        acc = state.get("acc", jnp.zeros((TOK, 128), F32))
        for f in range(first, last):
            centered = text_all[f].astype(F32) - state["mean"]
            normed = (centered * state["scale"] * gain_ref[:, f * 256 : (f + 1) * 256] + bias_ref[:, f * 256 : (f + 1) * 256]).astype(BF16)
            acc = acc + jnp.dot(normed, wq_ref[f * 256 : (f + 1) * 256, :], preferred_element_type=F32)
        state["acc"] = acc

    todo = {}

    def at_turn(turn, action, *args):
        todo.setdefault(turn, []).append(functools.partial(action, *args))

    for k in range(1, HALF_Y + 1):
        at_turn(2 * k - 1, text_ring.step, k)
        at_turn(2 * k + 10, cot_ring.step, k)
    at_turn(2, own_weight.start)
    for at, index in enumerate([7, 8, 9, 5, 6, 10, 3, 4, 11, 12, 1, 2, 13, 14, 0]):
        at_turn(4 + at // 4, send_weight, index)
    at_turn(7, cot_ring.begin)
    at_turn(9, query_load.wait)
    at_turn(10, norm_mean)
    at_turn(11, norm_scale)
    at_turn(13, project, 0, 8)
    at_turn(15, project, 8, 16)
    at_turn(14, spread_weight)

    deliver(pairs_ref, 0)
    turn = 0
    for k in range(1, HALF_Z + 1):
        for ch in range(CHUNKS):
            for d in range(2):
                if exists(d, k, ch):
                    zcopies[d, k, ch].wait_recv()
                    if k < HALF_Z and exists(d, k + 1, ch):
                        hop(d, k + 1, ch)
            for action in todo.get(turn, ()):
                action()
            turn += 1
        deliver(held[0][k], k)
        if k < HALF_Z:
            deliver(held[1][k], NZ - k)

    queries = (state["acc"] * 128 ** (-0.5)).astype(BF16)
    cot_ring.finish()
    for copy in xcopies:
        copy.wait_recv()
    square = (LAT, LAT)
    diagonal = lax.broadcasted_iota(jnp.int32, square, 0) == lax.broadcasted_iota(jnp.int32, square, 1)
    column = (lax.broadcasted_iota(jnp.int32, (LAT, 5 * LAT), 1) // LAT).astype(F32)
    for s in range(3):
        rows = slice(s * LAT, (s + 1) * LAT)
        blocks = [kv_ref[index_ref[k, 3 * x + s]] for k in range(5)]
        keys = jnp.concatenate([b[:, :128] for b in blocks], axis=0)
        values = jnp.concatenate([b[:, 128:] for b in blocks], axis=0)
        scores = lax.dot_general(queries[rows], keys, (((1,), (1,)), ((), ())), preferred_element_type=F32)
        pos = jnp.sum(jnp.where(diagonal, pos_ref[s : s + 1, :].astype(F32), 0.0), axis=1, keepdims=True)
        scores = jnp.where(pos == column, scores, -1e30)
        weights = jnp.exp(scores - jnp.max(scores, axis=-1, keepdims=True))
        probs = (weights / jnp.sum(weights, axis=-1, keepdims=True)).astype(BF16)
        mixed = jnp.dot(probs, values, preferred_element_type=F32)
        ctx_ref[rows, :] = jnp.where(pos >= 0, mixed, 0.0).astype(BF16)

    zpeers = [{"z": lax.rem(z + kk, NZ)} for kk in range(NZ)]
    xpeers = x_peers(x)
    partner = {"c": 1 - c}
    context = ctx_ref[...]
    gcopies = {}
    ycopies = {}
    pcopies = {}
    first = True
    for kk in FAR_FIRST:
        block = cot_all[lax.rem(z + kk, NZ)]
        product[kk] = lax.dot_general(block, context, (((0,), (0,)), ((), ())), preferred_element_type=F32)
        for dx in (1, 2, 3, 0):
            part = product[kk, pl.ds(pl.multiple_of(lax.rem(x + dx, NX) * 64, 64), 64), :]
            if dx == 0:
                own[kk] = part
            else:
                gsend[dx - 1, kk] = part.astype(BF16)
                gcopies[dx, kk] = go(
                    remote(
                        gsend.at[dx - 1, kk],
                        grecv.at[dx - 1, kk],
                        xs.at[dx - 1, kk],
                        xr.at[dx - 1, kk],
                        xpeers[dx - 1],
                    )
                )
        if first:
            first = False
            for dy in (4, 3, 5, 2, 6, 1, 7):
                ycopies[dy] = go(
                    remote(ctx_ref, same.at[dy], ys.at[dy], yr.at[dy], {"y": lax.rem(y + dy, NY)})
                )
            pcopies[0] = go(remote(ctx_ref, other.at[0], ps.at[0], pr.at[0], partner))

    def pass_on(dy):
        ycopies[dy].wait_recv()
        pcopies[dy] = go(remote(same.at[dy], other.at[dy], ps.at[dy], pr.at[dy], partner))

    near = [1, 7, 2, 6, 3, 5, 4]
    hcopies = {}
    for at, kk in enumerate(FAR_FIRST):
        total = own[kk]
        for dx in range(1, NX):
            gcopies[dx, kk].wait_recv()
            total = total + grecv[dx - 1, kk].astype(F32)
        if kk == 0:
            own[0] = total
        else:
            hsend[kk] = total.astype(BF16)
            hcopies[kk] = go(remote(hsend.at[kk], hrecv.at[kk], zs.at[kk], zr.at[kk], zpeers[kk]))
        if at % 2 == 1 and near:
            pass_on(near.pop(0))
    weight_spread()
    gate = gate_ref[0]
    update = jnp.zeros((TOK, 256), F32)
    for dy in (0, 1, 7, 2, 6, 3, 5, 4):
        row = 2 * lax.rem(y + NY - dy, NY)
        mine = context if dy == 0 else same[dy]
        update = update + jnp.dot(mine, wo_all[row + c], preferred_element_type=F32)
        pcopies[dy].wait_recv()
        update = update + jnp.dot(other[dy], wo_all[row + 1 - c], preferred_element_type=F32)
    out_ref[...] = (text_all[me].astype(F32) + gate * update).astype(BF16)
    total = own[0]
    for kk in FAR_FIRST[::-1][1:]:
        hcopies[kk].wait_recv()
        total = total + hrecv[kk].astype(F32)
    grad_ref[...] = gate * total
    for copy in started:
        copy.wait_send()


def fused_call(sel, index, gate, latents, wl, text, cot, wo, wq, gain, bias, pos):
    vmem = pl.BlockSpec(memory_space=pltpu.VMEM)
    smem = pl.BlockSpec(memory_space=pltpu.SMEM)
    dma = pltpu.SemaphoreType.DMA
    ring = [dma((2, HALF_Y + 1)), dma((2, HALF_Y + 1)), dma((NY + 1,)), dma((NY,))]
    return pl.pallas_call(
        fused_kernel,
        out_shape=(jax.ShapeDtypeStruct((TOK, 256), BF16), jax.ShapeDtypeStruct((64, 128), F32)),
        in_specs=[smem] * 3 + [pl.BlockSpec(memory_space=pltpu.HBM)] * 6 + [vmem] * 3,
        out_specs=(vmem, vmem),
        scratch_shapes=[
            pltpu.VMEM((GROUP * 256, 256), BF16),
            pltpu.VMEM((GROUP * 256, 128), BF16),
            pltpu.VMEM((IMG * LAT, GROUP * 256), BF16),
            pltpu.VMEM((IMG * LAT, 256), BF16),
            pltpu.VMEM((NX * NZ, LAT, 256), BF16),
            pltpu.VMEM((GROUP, TOK, 256), BF16),
            pltpu.VMEM((GROUP, TOK, 256), BF16),
            pltpu.VMEM((GROUP, 128, 256), BF16),
            pltpu.VMEM((NX - 1, NZ, LAT, 256), BF16),
            pltpu.VMEM((TOK, 128), BF16),
            pltpu.VMEM((NZ, 256, 128), F32),
            pltpu.VMEM((NZ, 64, 128), F32),
            pltpu.VMEM((NX - 1, NZ, 64, 128), BF16),
            pltpu.VMEM((NX - 1, NZ, 64, 128), BF16),
            pltpu.VMEM((NZ, 64, 128), BF16),
            pltpu.VMEM((NZ, 64, 128), BF16),
            pltpu.VMEM((NY, TOK, 128), BF16),
            pltpu.VMEM((NY, TOK, 128), BF16),
            dma((CHUNKS + 3,)),
            dma((2, HALF_Z + 1, CHUNKS)),
            dma((2, HALF_Z + 1, CHUNKS)),
            dma((NX - 1, NZ)),
            dma((NX - 1, NZ)),
            *ring,
            *ring,
            dma((GROUP - 1,)),
            dma((GROUP - 1,)),
            dma((NX,)),
            dma((NX,)),
            dma((NX - 1, NZ)),
            dma((NX - 1, NZ)),
            dma((NZ,)),
            dma((NZ,)),
            dma((NY,)),
            dma((NY,)),
            dma((NY,)),
            dma((NY,)),
        ]
        + [pltpu.VMEM((IMG * LAT, 256), BF16)] * (NZ - 1),
        compiler_params=pltpu.CompilerParams(
            collective_id=0, has_side_effects=True, vmem_limit_bytes=62 << 20
        ),
        name="fused",
    )(sel, index, gate, latents, wl, text, cot, wo, wq, gain, bias, pos)


def routes(media_refs, owner_map, z, x):
    refs = lax.dynamic_slice_in_dim(media_refs.T, 12 * z, 12, 1)
    lookup = jnp.maximum(refs, 0)[:, :, None] == jnp.arange(owner_map.shape[0], dtype=jnp.int32)
    storage = jnp.sum(jnp.where(lookup, owner_map, 0), axis=-1)
    owner, within = storage // IMG, storage % IMG
    dz = (z + NZ - owner // NX) % NZ
    source_x = owner % NX
    dest_dx = (jnp.arange(12, dtype=jnp.int32) // 3 + NX - x) % NX
    cell = jnp.arange(NZ * NX, dtype=jnp.int32)[:, None, None]
    hit = (refs >= 0) & (source_x == x) & (dz * NX + dest_dx == cell)
    sel = jnp.sum(jnp.where(hit, within, 0), axis=(1, 2))
    index = ((x + NX - source_x) % NX) * NZ + dz
    return sel, index


def body(
    text_states,
    cotangent,
    norm_gain,
    norm_bias,
    branch_gate,
    query_weight,
    latent_weight,
    output_weight,
    latents,
    media_refs,
    media_pos,
    owner_map,
):
    sel, index = routes(media_refs, owner_map, lax.axis_index("z"), lax.axis_index("x"))
    layer_out, out_grad = fused_call(
        sel,
        index,
        jnp.tanh(branch_gate),
        latents.reshape(IMG * LAT, -1),
        latent_weight.reshape(-1, 256),
        text_states.reshape(TOK, 256),
        cotangent.reshape(TOK, 256),
        output_weight.reshape(128, -1),
        query_weight.reshape(-1, 128),
        norm_gain.reshape(1, -1),
        norm_bias.reshape(1, -1),
        media_pos,
    )
    return layer_out.reshape(3, 64, 256), jnp.transpose(out_grad, (1, 0))[None]


def solution(mesh):
    split = Mesh(mesh.devices.reshape(NZ, NX, NY, 2), ("z", "x", "y", "c"))
    dp, fsdp = ("z", "x"), ("y", "c")
    return jax.shard_map(
        body,
        mesh=split,
        in_specs=(
            P(dp, None, fsdp),
            P(dp, None, fsdp),
            P(),
            P(),
            P(),
            P(None, fsdp, None),
            P(None, fsdp, None),
            P(fsdp, None, None),
            P(dp, None, None),
            P(),
            P(dp, None),
            P(),
        ),
        out_specs=(P(dp, None, fsdp), P(fsdp, None, dp)),
        check_vma=False,
    )
```

time: 136 us -> 113 us (0.83)
  the two profiles are of different devices: /device:TPU:8 before, /device:TPU:1 now
where the time goes in v2:
time: 113 us
  Pallas kernels  105 us (93%)
  other arithmetic  3.76 us (3%)
  local copies, waits for them, and re-layouts  2.91 us (3%)
  between operations  1.34 us (1%)
    pallas_call x1, Pallas kernels, fused_call(): pl.pallas_call(fused_kernel, out_shape=(jax.ShapeDtypeStruct((TOK, 256),...  105 us
    unnamed x2, local copies, waits for them, and re-layouts  2.91 us

profile of v2, /device:TPU:1, one launch (start us, length us, event | category | flops | bytes accessed | tf_op | source)
XLA Modules:
  0.0 113.0 jit_solution(14091225017998136454)
XLA Ops:
  1.3 0.8 maximum_bitcast_fusion
  2.1 0.9 select_reduce_fusion
  3.1 0.8 bitcast_and_fusion
  3.8 0.6 fusion.5
  4.5 0.6 select_reduce_fusion.1.sel_ref
  5.1 105.0 %fused.1 = (bf16[192,256]{1,0:T(8,128)(2,1)}, f32[64,128]{1,0:T(8,128)}) custom-call(s32[64]{0:T(128)} %select_reduce_fusion.1.sel_ref, s32[5,12]{1,0:T(8,128)} %get-tuple-element.6.index_ref, f32[1]{0:T(128)S(6)} %tanh.3.gate_ref, bf16[576,4096]{1,0:T(8,128)(2,1)} %bitcast.16, bf16[4096,256]{1,0:T(8,128)(2,1)} %bitcast.17, bf16[192,256]{1,0:T(8,128)(2,1)} %bitcast.20, ...), custom_call_target="tpu_custom_call" | custom-call | tf_op jit(solution)/shard_map/fused/pallas_call | solution.py:460
  110.1 1.5 %copy.17 = bf16[3,64,256]{2,1,0:T(8,128)(2,1)} copy(bf16[3,64,256]{2,1,0:T(8,128)(2,1)} %bitcast.22) | data formatting | bytes 196608
  111.6 1.4 %copy.18 = f32[1,128,64]{1,2,0:T(8,128)} copy(f32[1,128,64]{1,2,0:T(8,128)} %bitcast.23) | data formatting | bytes 65536
  (1 shorter events, 0.0 us)

commit v3 on v2

--- a/solution.py
+++ b/solution.py
@@ -16,7 +16,8 @@
 LAT = 64
 TOK = 192
 CHUNKS = 3
-CHUNK_ROWS = IMG * LAT // CHUNKS
+CHUNK_IMG = IMG // CHUNKS
+CHUNK_ROWS = CHUNK_IMG * LAT
 QUARTER = 128 // NX
 HALF_Z = NZ // 2
 HALF_Y = NY // 2
@@ -114,8 +115,8 @@
 
 
 def fused_kernel(
-    sel_ref,
-    index_ref,
+    refs_ref,
+    owner_ref,
     gate_ref,
     latents_ref,
     wl_hbm,
@@ -137,6 +138,8 @@
     cot_all,
     wo_all,
     picked,
+    far_picked,
+    stored,
     ctx_ref,
     product,
     own,
@@ -151,6 +154,8 @@
     zrecv,
     xsend,
     xrecv,
+    fsend,
+    frecv,
     tsend,
     trecv,
     tpsend,
@@ -197,20 +202,34 @@
         started.append(copy)
         return copy
 
-    held = ([pairs_ref, *slots[:HALF_Z]], [pairs_ref, *slots[HALF_Z:]] + [slots[HALF_Z - 1]])
-
-    def exists(direction, k, ch):
-        return k < HALF_Z or (k == HALF_Z and (ch == CHUNKS - 1) == (direction == 1))
+    held = ([pairs_ref, *slots[: HALF_Z - 1]], [pairs_ref, *slots[HALF_Z - 1 :]])
 
     def zcopy(direction, k, ch):
+        images = pl.ds(ch * CHUNK_IMG, CHUNK_IMG)
         return remote(
-            held[direction][k - 1].at[chunk_rows(ch)],
-            held[direction][k].at[chunk_rows(ch)],
+            held[direction][k - 1].at[images],
+            held[direction][k].at[images],
             zsend.at[direction, k, ch],
             zrecv.at[direction, k, ch],
             ups[direction],
         )
 
+    def find(place, plane, dx):
+        first = 3 * (NX * plane + lax.rem(x + dx, NX))
+        for s in range(3):
+            for k in range(5):
+                ref = refs_ref[k, first + s]
+                row = owner_ref[jnp.maximum(ref, 0)]
+                stored[place * 15 + s * 5 + k] = jnp.where(ref >= 0, row, -1000)
+
+    def within(place, plane):
+        base = IMG * (NX * plane + x)
+        wanted = 0
+        for e in range(15):
+            at = stored[place * 15 + e] - base
+            wanted = wanted + jnp.where((at >= 0) & (at < IMG), at, 0)
+        return wanted
+
     zcopies = {}
 
     def hop(direction, k, ch):
@@ -219,12 +238,16 @@
     text_ring = YRing(text_ref, text_all, y, c, tsend, trecv, tpsend, tprecv)
     cot_ring = YRing(cot_ref, cot_all, y, c, csend, crecv, cpsend, cprecv)
 
+    for dx in range(NX):
+        find(dx, z, dx)
     weight_load.wait()
     for ch in range(CHUNKS):
         loads[ch].wait()
-        pairs_ref[chunk_rows(ch), :] = jnp.dot(
-            lat[chunk_rows(ch), :], wl_ref[...], preferred_element_type=F32
-        ).astype(BF16)
+        pairs_ref[ch * CHUNK_IMG : (ch + 1) * CHUNK_IMG] = (
+            jnp.dot(lat[chunk_rows(ch), :], wl_ref[...], preferred_element_type=F32)
+            .astype(BF16)
+            .reshape(CHUNK_IMG, LAT, 256)
+        )
         if ch == 0:
             wait_peers()
             text_ring.begin()
@@ -235,10 +258,7 @@
 
     def deliver(block, kk):
         for dx in (1, 2, 3, 0):
-            wanted = sel_ref[kk * NX + dx]
-            image = block[:LAT, :]
-            for i in range(1, IMG):
-                image = jnp.where(wanted == i, block[i * LAT : (i + 1) * LAT, :], image)
+            image = block[within(dx, lax.rem(z + NZ - kk, NZ))]
             if dx == 0:
                 kv_ref[kk] = image
             else:
@@ -255,6 +275,30 @@
                     )
                 )
 
+    far_up, far_down = lax.rem(z + NZ - HALF_Z + 1, NZ), lax.rem(z + HALF_Z - 1, NZ)
+    far = [(1, 0, far_up), (2, 0, far_up), (3, 1, far_down), (0, 1, far_down)]
+    far_copies = []
+
+    def find_far():
+        for dx, direction, _ in far:
+            find(NX + dx, ups[direction]["z"], dx)
+
+    def deliver_far():
+        for dx, direction, source in far:
+            far_picked[dx] = held[direction][HALF_Z - 1][within(NX + dx, source)]
+            where = {"z": ups[direction]["z"], "x": lax.rem(x + dx, NX)}
+            far_copies.append(
+                go(
+                    remote(
+                        far_picked.at[dx],
+                        kv_ref.at[dx * NZ + HALF_Z],
+                        fsend.at[dx],
+                        frecv.at[dx],
+                        where if dx else ups[direction],
+                    )
+                )
+            )
+
     def fsdp_place(index, sign):
         if index == 0:
             return y, 1 - c
@@ -345,32 +389,39 @@
     at_turn(15, project, 8, 16)
     at_turn(14, spread_weight)
 
+    at_turn(16, find_far)
     deliver(pairs_ref, 0)
     turn = 0
-    for k in range(1, HALF_Z + 1):
+    for k in range(1, HALF_Z):
         for ch in range(CHUNKS):
             for d in range(2):
-                if exists(d, k, ch):
-                    zcopies[d, k, ch].wait_recv()
-                    if k < HALF_Z and exists(d, k + 1, ch):
-                        hop(d, k + 1, ch)
+                zcopies[d, k, ch].wait_recv()
+                if k < HALF_Z - 1:
+                    hop(d, k + 1, ch)
             for action in todo.get(turn, ()):
                 action()
             turn += 1
+        if k == HALF_Z - 1:
+            deliver_far()
         deliver(held[0][k], k)
-        if k < HALF_Z:
-            deliver(held[1][k], NZ - k)
+        deliver(held[1][k], NZ - k)
 
     queries = (state["acc"] * 128 ** (-0.5)).astype(BF16)
     cot_ring.finish()
-    for copy in xcopies:
+    for copy in [*xcopies, *far_copies]:
         copy.wait_recv()
+
+    def arrival(entry):
+        owner = lax.div(jnp.maximum(stored[entry], 0), IMG)
+        from_x = lax.rem(x + NX - lax.rem(owner, NX), NX)
+        return from_x * NZ + lax.rem(z + NZ - lax.div(owner, NX), NZ)
+
     square = (LAT, LAT)
     diagonal = lax.broadcasted_iota(jnp.int32, square, 0) == lax.broadcasted_iota(jnp.int32, square, 1)
     column = (lax.broadcasted_iota(jnp.int32, (LAT, 5 * LAT), 1) // LAT).astype(F32)
     for s in range(3):
         rows = slice(s * LAT, (s + 1) * LAT)
-        blocks = [kv_ref[index_ref[k, 3 * x + s]] for k in range(5)]
+        blocks = [kv_ref[arrival(s * 5 + k)] for k in range(5)]
         keys = jnp.concatenate([b[:, :128] for b in blocks], axis=0)
         values = jnp.concatenate([b[:, 128:] for b in blocks], axis=0)
         scores = lax.dot_general(queries[rows], keys, (((1,), (1,)), ((), ())), preferred_element_type=F32)
@@ -452,7 +503,7 @@
         copy.wait_send()
 
 
-def fused_call(sel, index, gate, latents, wl, text, cot, wo, wq, gain, bias, pos):
+def fused_call(refs, owner, gate, latents, wl, text, cot, wo, wq, gain, bias, pos):
     vmem = pl.BlockSpec(memory_space=pltpu.VMEM)
     smem = pl.BlockSpec(memory_space=pltpu.SMEM)
     dma = pltpu.SemaphoreType.DMA
@@ -466,12 +517,14 @@
             pltpu.VMEM((GROUP * 256, 256), BF16),
             pltpu.VMEM((GROUP * 256, 128), BF16),
             pltpu.VMEM((IMG * LAT, GROUP * 256), BF16),
-            pltpu.VMEM((IMG * LAT, 256), BF16),
+            pltpu.VMEM((IMG, LAT, 256), BF16),
             pltpu.VMEM((NX * NZ, LAT, 256), BF16),
             pltpu.VMEM((GROUP, TOK, 256), BF16),
             pltpu.VMEM((GROUP, TOK, 256), BF16),
             pltpu.VMEM((GROUP, 128, 256), BF16),
             pltpu.VMEM((NX - 1, NZ, LAT, 256), BF16),
+            pltpu.VMEM((NX, LAT, 256), BF16),
+            pltpu.SMEM((2 * NX * 15,), jnp.int32),
             pltpu.VMEM((TOK, 128), BF16),
             pltpu.VMEM((NZ, 256, 128), F32),
             pltpu.VMEM((NZ, 64, 128), F32),
@@ -482,10 +535,12 @@
             pltpu.VMEM((NY, TOK, 128), BF16),
             pltpu.VMEM((NY, TOK, 128), BF16),
             dma((CHUNKS + 3,)),
-            dma((2, HALF_Z + 1, CHUNKS)),
-            dma((2, HALF_Z + 1, CHUNKS)),
+            dma((2, HALF_Z, CHUNKS)),
+            dma((2, HALF_Z, CHUNKS)),
             dma((NX - 1, NZ)),
             dma((NX - 1, NZ)),
+            dma((NX,)),
+            dma((NX,)),
             *ring,
             *ring,
             dma((GROUP - 1,)),
@@ -501,27 +556,12 @@
             dma((NY,)),
             dma((NY,)),
         ]
-        + [pltpu.VMEM((IMG * LAT, 256), BF16)] * (NZ - 1),
+        + [pltpu.VMEM((IMG, LAT, 256), BF16)] * (2 * (HALF_Z - 1)),
         compiler_params=pltpu.CompilerParams(
             collective_id=0, has_side_effects=True, vmem_limit_bytes=62 << 20
         ),
         name="fused",
-    )(sel, index, gate, latents, wl, text, cot, wo, wq, gain, bias, pos)
-
-
-def routes(media_refs, owner_map, z, x):
-    refs = lax.dynamic_slice_in_dim(media_refs.T, 12 * z, 12, 1)
-    lookup = jnp.maximum(refs, 0)[:, :, None] == jnp.arange(owner_map.shape[0], dtype=jnp.int32)
-    storage = jnp.sum(jnp.where(lookup, owner_map, 0), axis=-1)
-    owner, within = storage // IMG, storage % IMG
-    dz = (z + NZ - owner // NX) % NZ
-    source_x = owner % NX
-    dest_dx = (jnp.arange(12, dtype=jnp.int32) // 3 + NX - x) % NX
-    cell = jnp.arange(NZ * NX, dtype=jnp.int32)[:, None, None]
-    hit = (refs >= 0) & (source_x == x) & (dz * NX + dest_dx == cell)
-    sel = jnp.sum(jnp.where(hit, within, 0), axis=(1, 2))
-    index = ((x + NX - source_x) % NX) * NZ + dz
-    return sel, index
+    )(refs, owner, gate, latents, wl, text, cot, wo, wq, gain, bias, pos)
 
 
 def body(
@@ -538,10 +578,9 @@
     media_pos,
     owner_map,
 ):
-    sel, index = routes(media_refs, owner_map, lax.axis_index("z"), lax.axis_index("x"))
     layer_out, out_grad = fused_call(
-        sel,
-        index,
+        media_refs.T,
+        owner_map,
         jnp.tanh(branch_gate),
         latents.reshape(IMG * LAT, -1),
         latent_weight.reshape(-1, 256),

time: 113 us -> 109 us (0.965)
  other arithmetic: 3.76 us -> 0 us
    reduce_sum x2 -> x0, other arithmetic: 1.56 us -> none  [the longest x1 0.93 us: routes(): storage = jnp.sum(jnp.where(lookup, owner_map, 0), axis=-1)]
where the time goes in v3:
time: 109 us
  Pallas kernels  105 us (96%)
  local copies, waits for them, and re-layouts  2.91 us (3%)
  between operations  1.33 us (1%)
    pallas_call x1, Pallas kernels, fused_call(): pl.pallas_call(fused_kernel, out_shape=(jax.ShapeDtypeStruct((TOK, 256),...  105 us
    unnamed x2, local copies, waits for them, and re-layouts  2.91 us

profile of v3, /device:TPU:1, one launch (start us, length us, event | category | flops | bytes accessed | tf_op | source)
XLA Modules:
  0.0 109.2 jit_solution(9732090532147358967)
XLA Ops:
  1.3 104.9 %fused.1 = (bf16[192,256]{1,0:T(8,128)(2,1)}, f32[64,128]{1,0:T(8,128)}) custom-call(s32[5,192]{1,0:T(8,128)} %bitcast.23, s32[576]{0:T(1024)} %owner_ref.1, f32[1]{0:T(128)S(6)} %tanh.3.gate_ref, bf16[576,4096]{1,0:T(8,128)(2,1)} %bitcast.13, bf16[4096,256]{1,0:T(8,128)(2,1)} %bitcast.14, bf16[192,256]{1,0:T(8,128)(2,1)} %bitcast.17, ...), custom_call_target="tpu_custom_call" | custom-call | tf_op jit(solution)/shard_map/fused/pallas_call | solution.py:511
  106.3 1.5 %copy.17 = bf16[3,64,256]{2,1,0:T(8,128)(2,1)} copy(bf16[3,64,256]{2,1,0:T(8,128)(2,1)} %bitcast.19) | data formatting | bytes 196608
  107.8 1.4 %copy.18 = f32[1,128,64]{1,2,0:T(8,128)} copy(f32[1,128,64]{1,2,0:T(8,128)} %bitcast.20) | data formatting | bytes 65536

commit v4 on v3

--- a/solution.py
+++ b/solution.py
@@ -192,8 +192,7 @@
     weight_load = pltpu.make_async_copy(wl_hbm, wl_ref, lsem.at[CHUNKS])
     query_load = pltpu.make_async_copy(wq_hbm, wq_ref, lsem.at[CHUNKS + 1])
     weight_load.start()
-    for load in [*loads, query_load]:
-        load.start()
+    loads[0].start()
     wait_peers = meet([*ups, *x_peers(x), *fsdp_peers(y, c)])
     started = []
 
@@ -241,6 +240,8 @@
     for dx in range(NX):
         find(dx, z, dx)
     weight_load.wait()
+    for load in loads[1:]:
+        load.start()
     for ch in range(CHUNKS):
         loads[ch].wait()
         pairs_ref[ch * CHUNK_IMG : (ch + 1) * CHUNK_IMG] = (
@@ -376,18 +377,19 @@
         todo.setdefault(turn, []).append(functools.partial(action, *args))
 
     for k in range(1, HALF_Y + 1):
-        at_turn(2 * k - 1, text_ring.step, k)
+        at_turn(2 * k, text_ring.step, k)
         at_turn(2 * k + 10, cot_ring.step, k)
     at_turn(2, own_weight.start)
+    at_turn(3, query_load.start)
     for at, index in enumerate([7, 8, 9, 5, 6, 10, 3, 4, 11, 12, 1, 2, 13, 14, 0]):
         at_turn(4 + at // 4, send_weight, index)
     at_turn(7, cot_ring.begin)
     at_turn(9, query_load.wait)
-    at_turn(10, norm_mean)
-    at_turn(11, norm_scale)
-    at_turn(13, project, 0, 8)
-    at_turn(15, project, 8, 16)
-    at_turn(14, spread_weight)
+    at_turn(11, norm_mean)
+    at_turn(13, norm_scale)
+    at_turn(15, project, 0, 8)
+    at_turn(17, project, 8, 16)
+    at_turn(13, spread_weight)
 
     at_turn(16, find_far)
     deliver(pairs_ref, 0)
@@ -470,7 +472,7 @@
         ycopies[dy].wait_recv()
         pcopies[dy] = go(remote(same.at[dy], other.at[dy], ps.at[dy], pr.at[dy], partner))
 
-    near = [1, 7, 2, 6, 3, 5, 4]
+    passing = {9: (4, 3, 5), 11: (2, 6), 13: (1, 7)}
     hcopies = {}
     for at, kk in enumerate(FAR_FIRST):
         total = own[kk]
@@ -482,15 +484,16 @@
         else:
             hsend[kk] = total.astype(BF16)
             hcopies[kk] = go(remote(hsend.at[kk], hrecv.at[kk], zs.at[kk], zr.at[kk], zpeers[kk]))
-        if at % 2 == 1 and near:
-            pass_on(near.pop(0))
+        for dy in passing.get(at, ()):
+            pass_on(dy)
     weight_spread()
     gate = gate_ref[0]
-    update = jnp.zeros((TOK, 256), F32)
-    for dy in (0, 1, 7, 2, 6, 3, 5, 4):
+    update = jnp.dot(context, wo_all[me], preferred_element_type=F32)
+    for dy in range(1, NY):
         row = 2 * lax.rem(y + NY - dy, NY)
-        mine = context if dy == 0 else same[dy]
-        update = update + jnp.dot(mine, wo_all[row + c], preferred_element_type=F32)
+        update = update + jnp.dot(same[dy], wo_all[row + c], preferred_element_type=F32)
+    for dy in (0, 4, 3, 5, 2, 6, 1, 7):
+        row = 2 * lax.rem(y + NY - dy, NY)
         pcopies[dy].wait_recv()
         update = update + jnp.dot(other[dy], wo_all[row + 1 - c], preferred_element_type=F32)
     out_ref[...] = (text_all[me].astype(F32) + gate * update).astype(BF16)

time: 109 us -> 107 us (0.982)
  Pallas kernels: 105 us -> 103 us
    pallas_call x1, Pallas kernels: 105 us -> 103 us  [fused_call(): pl.pallas_call(fused_kernel, out_shape=(jax.ShapeDtypeStruct((TOK, 256),...]
where the time goes in v4:
time: 107 us
  Pallas kernels  103 us (96%)
  local copies, waits for them, and re-layouts  2.91 us (3%)
  between operations  1.33 us (1%)
    pallas_call x1, Pallas kernels, fused_call(): pl.pallas_call(fused_kernel, out_shape=(jax.ShapeDtypeStruct((TOK, 256),...  103 us
    unnamed x2, local copies, waits for them, and re-layouts  2.91 us

profile of v4, /device:TPU:1, one launch (start us, length us, event | category | flops | bytes accessed | tf_op | source)
XLA Modules:
  0.0 107.0 jit_solution(8205969209078051239)
XLA Ops:
  1.3 102.7 %fused.1 = (bf16[192,256]{1,0:T(8,128)(2,1)}, f32[64,128]{1,0:T(8,128)}) custom-call(s32[5,192]{1,0:T(8,128)} %bitcast.23, s32[576]{0:T(1024)} %owner_ref.1, f32[1]{0:T(128)S(6)} %tanh.3.gate_ref, bf16[576,4096]{1,0:T(8,128)(2,1)} %bitcast.13, bf16[4096,256]{1,0:T(8,128)(2,1)} %bitcast.14, bf16[192,256]{1,0:T(8,128)(2,1)} %bitcast.17, ...), custom_call_target="tpu_custom_call" | custom-call | tf_op jit(solution)/shard_map/fused/pallas_call | solution.py:514
  104.1 1.5 %copy.17 = bf16[3,64,256]{2,1,0:T(8,128)(2,1)} copy(bf16[3,64,256]{2,1,0:T(8,128)(2,1)} %bitcast.19) | data formatting | bytes 196608
  105.6 1.4 %copy.18 = f32[1,128,64]{1,2,0:T(8,128)} copy(f32[1,128,64]{1,2,0:T(8,128)} %bitcast.20) | data formatting | bytes 65536

commit v5 on v4

--- a/solution.py
+++ b/solution.py
@@ -19,6 +19,7 @@
 CHUNK_IMG = IMG // CHUNKS
 CHUNK_ROWS = CHUNK_IMG * LAT
 QUARTER = 128 // NX
+BEHIND = 6
 HALF_Z = NZ // 2
 HALF_Y = NY // 2
 BF16 = jnp.bfloat16
@@ -257,9 +258,14 @@
 
     xcopies = []
 
+    choices = {}
+
+    def choose(kk):
+        choices[kk] = [within(dx, lax.rem(z + NZ - kk, NZ)) for dx in range(NX)]
+
     def deliver(block, kk):
         for dx in (1, 2, 3, 0):
-            image = block[within(dx, lax.rem(z + NZ - kk, NZ))]
+            image = block[choices[kk][dx]]
             if dx == 0:
                 kv_ref[kk] = image
             else:
@@ -284,9 +290,12 @@
         for dx, direction, _ in far:
             find(NX + dx, ups[direction]["z"], dx)
 
+    def choose_far():
+        choices["far"] = {dx: within(NX + dx, source) for dx, _, source in far}
+
     def deliver_far():
-        for dx, direction, source in far:
-            far_picked[dx] = held[direction][HALF_Z - 1][within(NX + dx, source)]
+        for dx, direction, _ in far:
+            far_picked[dx] = held[direction][HALF_Z - 1][choices["far"][dx]]
             where = {"z": ups[direction]["z"], "x": lax.rem(x + dx, NX)}
             far_copies.append(
                 go(
@@ -391,7 +400,19 @@
     at_turn(17, project, 8, 16)
     at_turn(13, spread_weight)
 
+    def arrival(entry):
+        owner = lax.div(jnp.maximum(stored[entry], 0), IMG)
+        from_x = lax.rem(x + NX - lax.rem(owner, NX), NX)
+        return from_x * NZ + lax.rem(z + NZ - lax.div(owner, NX), NZ)
+
+    arrivals = []
+    at_turn(19, lambda: arrivals.extend(arrival(entry) for entry in range(15)))
     at_turn(16, find_far)
+    at_turn(18, choose_far)
+    for k in range(1, HALF_Z):
+        at_turn(3 * k - 3, choose, k)
+        at_turn(3 * k - 3, choose, NZ - k)
+    choose(0)
     deliver(pairs_ref, 0)
     turn = 0
     for k in range(1, HALF_Z):
@@ -413,17 +434,12 @@
     for copy in [*xcopies, *far_copies]:
         copy.wait_recv()
 
-    def arrival(entry):
-        owner = lax.div(jnp.maximum(stored[entry], 0), IMG)
-        from_x = lax.rem(x + NX - lax.rem(owner, NX), NX)
-        return from_x * NZ + lax.rem(z + NZ - lax.div(owner, NX), NZ)
-
     square = (LAT, LAT)
     diagonal = lax.broadcasted_iota(jnp.int32, square, 0) == lax.broadcasted_iota(jnp.int32, square, 1)
     column = (lax.broadcasted_iota(jnp.int32, (LAT, 5 * LAT), 1) // LAT).astype(F32)
     for s in range(3):
         rows = slice(s * LAT, (s + 1) * LAT)
-        blocks = [kv_ref[arrival(s * 5 + k)] for k in range(5)]
+        blocks = [kv_ref[arrivals[s * 5 + k]] for k in range(5)]
         keys = jnp.concatenate([b[:, :128] for b in blocks], axis=0)
         values = jnp.concatenate([b[:, 128:] for b in blocks], axis=0)
         scores = lax.dot_general(queries[rows], keys, (((1,), (1,)), ((), ())), preferred_element_type=F32)
@@ -441,8 +457,8 @@
     gcopies = {}
     ycopies = {}
     pcopies = {}
-    first = True
-    for kk in FAR_FIRST:
+
+    def send_parts(kk):
         block = cot_all[lax.rem(z + kk, NZ)]
         product[kk] = lax.dot_general(block, context, (((0,), (0,)), ((), ())), preferred_element_type=F32)
         for dx in (1, 2, 3, 0):
@@ -460,21 +476,21 @@
                         xpeers[dx - 1],
                     )
                 )
-        if first:
-            first = False
-            for dy in (4, 3, 5, 2, 6, 1, 7):
-                ycopies[dy] = go(
-                    remote(ctx_ref, same.at[dy], ys.at[dy], yr.at[dy], {"y": lax.rem(y + dy, NY)})
-                )
-            pcopies[0] = go(remote(ctx_ref, other.at[0], ps.at[0], pr.at[0], partner))
+
+    def send_context():
+        for dy in (4, 3, 5, 2, 6, 1, 7):
+            ycopies[dy] = go(
+                remote(ctx_ref, same.at[dy], ys.at[dy], yr.at[dy], {"y": lax.rem(y + dy, NY)})
+            )
+        pcopies[0] = go(remote(ctx_ref, other.at[0], ps.at[0], pr.at[0], partner))
 
     def pass_on(dy):
         ycopies[dy].wait_recv()
         pcopies[dy] = go(remote(same.at[dy], other.at[dy], ps.at[dy], pr.at[dy], partner))
 
-    passing = {9: (4, 3, 5), 11: (2, 6), 13: (1, 7)}
     hcopies = {}
-    for at, kk in enumerate(FAR_FIRST):
+
+    def send_sum(kk):
         total = own[kk]
         for dx in range(1, NX):
             gcopies[dx, kk].wait_recv()
@@ -484,8 +500,17 @@
         else:
             hsend[kk] = total.astype(BF16)
             hcopies[kk] = go(remote(hsend.at[kk], hrecv.at[kk], zs.at[kk], zr.at[kk], zpeers[kk]))
-        for dy in passing.get(at, ()):
-            pass_on(dy)
+
+    passing = {9: (4, 3, 5), 11: (2, 6), 13: (1, 7)}
+    for at in range(NZ + BEHIND):
+        if at < NZ:
+            send_parts(FAR_FIRST[at])
+        if at == 0:
+            send_context()
+        if at >= BEHIND:
+            send_sum(FAR_FIRST[at - BEHIND])
+            for dy in passing.get(at - BEHIND, ()):
+                pass_on(dy)
     weight_spread()
     gate = gate_ref[0]
     update = jnp.dot(context, wo_all[me], preferred_element_type=F32)

time: 107 us -> 105 us (0.981)
  Pallas kernels: 103 us -> 101 us
    pallas_call x1, Pallas kernels: 103 us -> 101 us  [fused_call(): pl.pallas_call(fused_kernel, out_shape=(jax.ShapeDtypeStruct((TOK, 256),...]
where the time goes in v5:
time: 105 us
  Pallas kernels  101 us (96%)
  local copies, waits for them, and re-layouts  2.91 us (3%)
  between operations  1.33 us (1%)
    pallas_call x1, Pallas kernels, fused_call(): pl.pallas_call(fused_kernel, out_shape=(jax.ShapeDtypeStruct((TOK, 256),...  101 us
    unnamed x2, local copies, waits for them, and re-layouts  2.91 us

profile of v5, /device:TPU:1, one launch (start us, length us, event | category | flops | bytes accessed | tf_op | source)
XLA Modules:
  0.0 105.0 jit_solution(3218158143151767014)
XLA Ops:
  1.3 100.8 %fused.1 = (bf16[192,256]{1,0:T(8,128)(2,1)}, f32[64,128]{1,0:T(8,128)}) custom-call(s32[5,192]{1,0:T(8,128)} %bitcast.23, s32[576]{0:T(1024)} %owner_ref.1, f32[1]{0:T(128)S(6)} %tanh.3.gate_ref, bf16[576,4096]{1,0:T(8,128)(2,1)} %bitcast.13, bf16[4096,256]{1,0:T(8,128)(2,1)} %bitcast.14, bf16[192,256]{1,0:T(8,128)(2,1)} %bitcast.17, ...), custom_call_target="tpu_custom_call" | custom-call | tf_op jit(solution)/shard_map/fused/pallas_call | solution.py:539
  102.1 1.5 %copy.17 = bf16[3,64,256]{2,1,0:T(8,128)(2,1)} copy(bf16[3,64,256]{2,1,0:T(8,128)(2,1)} %bitcast.19) | data formatting | bytes 196608
  103.7 1.4 %copy.18 = f32[1,128,64]{1,2,0:T(8,128)} copy(f32[1,128,64]{1,2,0:T(8,128)} %bitcast.20) | data formatting | bytes 65536
